TPU v7x, 128 devices: a whole 4x4x4 slice. The times are simulated.
128 devices in a mesh: chaos: 8 (over z, core), space: 16 (over x, y).
Axes of the slice: x: 4, y: 4, z: 4, core: 2. Of those that a mesh axis runs over, the one named last changes fastest.
Arguments:
- panels: bfloat16 [216, 48, 2304], P('chaos', 'space'), may hold values from -6 to 6
- mean_field: float32 [48, 2304], P('space'), may hold values from 0.5 to 2
- fluctuations: float32 [6, 48, 2304], P(None, 'space'), may hold values from -1.5 to 1.5
- products: float32 [1218], replicated, may hold values from -4 to 4
- triples: int32 [1218, 3], replicated, may hold values from 0 to 209, as said below
- owner_slot: int32 [210], replicated, may hold values from 0 to 215, as said below
Outputs:
- first_apply: bfloat16 [216, 48, 2304], P('chaos', 'space')
- second_apply: bfloat16 [216, 48, 2304], P('chaos', 'space')
Inputs may be any that keep to these rules, and one draw needn't show every extreme that they name: `triples`: each row (i, j, k) names a nonzero of G_k; i and j are below 210, k below 7; repeated rows add; every chaos coefficient is some row's i and some row's j. `owner_slot`: distinct slots; slot s belongs to the group s // 27 along chaos.
All inputs are finite; a program needn't handle non-finite values.
Results may differ from a plain program's by a relative error of at most 0.007.
Values may be sent and summed in bfloat16 or wider, within the bound.
A program may use at most 64 MiB of HBM per device.

v0:
```python
import jax
import jax.numpy as jnp
from jax import lax
from jax.sharding import PartitionSpec as P

NXY = 48


scale_factor = 0.15


def padded(block, sides, width):
    for axis, dim in sides:
        count = lax.axis_size(axis)
        forward = [(i, i + 1) for i in range(count - 1)]
        backward = [(target, source) for source, target in forward]
        low = lax.ppermute(
            lax.slice_in_dim(block, block.shape[dim] - width, None, axis=dim), axis, forward
        )
        high = lax.ppermute(lax.slice_in_dim(block, 0, width, axis=dim), axis, backward)
        block = jnp.concatenate([low, block, high], axis=dim)
    return block


def shifted(source, offset, inside):
    length_last = source.shape[-1]
    padding = [(0, 0)] * (source.ndim - 1)
    if offset > 0:
        moved_values = jnp.pad(source[..., offset:], padding + [(0, offset)])
    else:
        moved_values = jnp.pad(source[..., : length_last + offset], padding + [(-offset, 0)])
    return jnp.where(inside, moved_values, jnp.zeros_like(moved_values))


def diffusion(extended, conductance_ext, side_cells):
    center = extended[..., 1:-1, :]
    conduct = conductance_ext[1:-1]
    flux_sum = 0.5 * (conduct + conductance_ext[2:]) * (center - extended[..., 2:, :])
    flux_sum = flux_sum + 0.5 * (conduct + conductance_ext[:-2]) * (center - extended[..., :-2, :])
    column = lax.iota(jnp.int32, center.shape[-1]) % side_cells
    everywhere = column >= 0
    for offset, inside in (
        (1, column < side_cells - 1),
        (-1, column > 0),
        (side_cells, everywhere),
        (-side_cells, everywhere),
    ):
        flux_sum = flux_sum + 0.5 * (conduct + shifted(conduct, offset, inside)) * (
            center - shifted(center, offset, inside)
        )
    return flux_sum


def shards(panels, mean_field, fluctuations, products, triples, owner_slot):
    own_count = panels.shape[0]
    slot_count = own_count * lax.axis_size("chaos")
    coefficients = jnp.concatenate([mean_field[None], fluctuations], axis=0)
    field_count = coefficients.shape[0]
    padded_coef = padded(coefficients, (("space", 1),), 1)
    row_slot = owner_slot[triples[:, 0]]
    column_slot = owner_slot[triples[:, 1]]
    tables = (
        jnp.zeros((field_count, slot_count, slot_count), jnp.float32)
        .at[triples[:, 2], row_slot, column_slot]
        .add(products)
    )
    tables = tables.astype(jnp.bfloat16)
    own_tables = lax.dynamic_slice_in_dim(tables, lax.axis_index("chaos") * own_count, own_count, 1)

    def combine(own_panels):
        summed = jnp.einsum(
            "krc,cpv->krpv",
            own_tables,
            lax.all_gather(own_panels, "chaos", axis=0, tiled=True),
            preferred_element_type=jnp.float32,
        )
        return summed.astype(jnp.bfloat16)

    def galerkin_apply(own_panels):
        combined = padded(combine(own_panels), (("space", 2),), 1)
        combined = lax.optimization_barrier(combined)
        result = jnp.zeros(own_panels.shape, jnp.float32)
        for field_index in range(field_count):
            result = result + diffusion(
                combined[field_index].astype(jnp.float32), padded_coef[field_index], NXY
            )
        return (scale_factor * result).astype(jnp.bfloat16)

    first_values = galerkin_apply(panels)
    second_values = galerkin_apply(first_values)
    return (first_values, second_values)


def solution(mesh):
    in_specs = (P("chaos", "space", None), P("space", None), P(None, "space", None), P(), P(), P())
    out_specs = (P("chaos", "space", None), P("chaos", "space", None))
    return jax.shard_map(shards, mesh=mesh, in_specs=in_specs, out_specs=out_specs, check_vma=False)
```

profile of v0, /device:TPU:7, one launch (start us, length us, event | category | flops | bytes accessed | tf_op | source)
XLA Modules:
  0.0 220.2 jit_solution(4822046470193139959)
XLA Ops:
  8.5 4.9 %collective-permute-start = (f32[7,1,2304]{2,1,0:T(1,128)S(1)}, f32[7,1,2304]{2,1,0:T(1,128)S(1)}, u32[]{:S(2)}, u32[]{:S(2)}) collective-permute-start(f32[7,1,2304]{2,1,0:T(1,128)S(1)} %get-tuple-element.94), channel_id=1, source_target_pairs={{1,0},{2,1},{3,2},{4,3},{5,4},{6,5},{7,6},{8,7},{9,8},{10,9},{11,1... | collective-permute-start | bytes 193544 | tf_op jit(solution)/shard_map/ppermute | solution.py:20
  13.4 1.9 collective-permute-start.3
  15.3 2.1 copy.8
  17.8 8.0 %gather_fusion.1 = s32[1218]{0:T(1024)S(1)} fusion(s32[210]{0:T(256)S(1)} %copy-done, s32[2048]{0:T(1024)S(1)} %get-tuple-element.162), kind=kCustom, calls=%fused_computation.1 | custom fusion | bytes 14616 | tf_op jit(solution)/shard_map/gather | solution.py:61
  25.8 8.0 %gather_fusion = s32[1218]{0:T(1024)S(1)} fusion(s32[210]{0:T(256)S(1)} %copy-done, s32[2048]{0:T(1024)S(1)} %get-tuple-element.163), kind=kCustom, calls=%fused_computation | custom fusion | bytes 14616 | tf_op jit(solution)/shard_map/gather | solution.py:60
  34.1 7.8 %scatter_custom_fusion = f32[326592]{0:T(1024)S(1)} fusion(s32[1218]{0:T(1024)S(1)} %broadcast_select_fusion, f32[1218]{0:T(1024)} %param.9, f32[]{:T(128)} %constant.69.clone.1), kind=kCustom, calls=%fused_computation.181 | custom fusion | flops 1218 | bytes 1306880
  41.9 2.5 %reshape.112 = bf16[7,216,216]{2,1,0:T(8,128)(2,1)S(1)} reshape(bf16[326592]{0:T(1024)(128)(2,1)S(1)} %convert_element_type.252) | data formatting | bytes 1306368 | tf_op jit(solution)/shard_map/convert_element_type | solution.py:67
  49.2 3.4 %all-gather.3.cloned.1.call-done = bf16[216,3,2304]{2,1,0:T(4,128)(2,1)} async-done(((bf16[27,3,2304]{2,1,0:T(4,128)(2,1)}), bf16[216,3,2304]{2,1,0:T(4,128)(2,1)}) %all-gather.3.cloned.1.call-update) | async-done | bytes 2986000 | tf_op jit(solution)/shard_map/all_gather | solution.py:74
  52.6 3.1 %convolution_convert_fusion.1 = bf16[7,27,3,2304]{3,1,2,0:T(8,128)(2,1)S(1)} fusion(bf16[216,3,2304]{2,1,0:T(4,128)(2,1)} %all-gather.3.cloned.1.call-done, bf16[7,216,216]{2,1,0:T(8,128)(2,1)S(1)} %reshape.112, s32[]{:T(128)S(6)} %select_n.521), kind=kOutput, calls=%fused_computation.6 | convolution fusion | flops 565657344 | bytes 5713412 | tf_op jit(solution)/shard_map/krc,cpv->krpv/dot_general | solution.py:71
  57.0 4.7 %collective-permute-start.2 = (bf16[7,27,1,2304]{3,0,2,1:T(8,128)(2,1)S(1)}, bf16[7,27,1,2304]{3,0,2,1:T(8,128)(2,1)S(1)}, u32[]{:S(2)}, u32[]{:S(2)}) collective-permute-start(bf16[7,27,1,2304]{3,0,2,1:T(8,128)(2,1)S(1)} %copy.11), channel_id=1, source_target_pairs={{1,0},{2,1},{3,2},{4,3},{5,4},{6,5},{7,6},{8,7},{9,8},{10,9},{11,1... | collective-permute-start | bytes 2612744 | tf_op jit(solution)/shard_map/ppermute | solution.py:20
  61.6 2.1 collective-permute-start.1
  64.7 18.0 %collective-permute-done.2 = bf16[7,27,1,2304]{3,0,2,1:T(8,128)(2,1)S(1)} collective-permute-done((bf16[7,27,1,2304]{3,0,2,1:T(8,128)(2,1)S(1)}, bf16[7,27,1,2304]{3,0,2,1:T(8,128)(2,1)S(1)}, u32[]{:S(2)}, u32[]{:S(2)}) %collective-permute-start.2) | collective-permute-done | bytes 870944 | tf_op jit(solution)/shard_map/ppermute | solution.py:20
  82.9 5.8 %collective-permute-done.1 = bf16[7,27,1,2304]{3,0,2,1:T(8,128)(2,1)S(1)} collective-permute-done((bf16[7,27,1,2304]{3,0,2,1:T(8,128)(2,1)S(1)}, bf16[7,27,1,2304]{3,0,2,1:T(8,128)(2,1)S(1)}, u32[]{:S(2)}, u32[]{:S(2)}) %collective-permute-start.1) | collective-permute-done | bytes 870944 | tf_op jit(solution)/shard_map/ppermute | solution.py:17
  100.1 1.6 fusion.197
  104.7 12.3 %fusion.69 = bf16[27,3,2304]{2,0,1:T(8,128)(2,1)} fusion(f32[27,5,2304]{2,0,1:T(8,128)S(1)} %get-tuple-element.12, f32[27,5,2304]{2,0,1:T(8,128)S(1)} %get-tuple-element.13, f32[27,5,2304]{2,0,1:T(8,128)S(1)} %get-tuple-element.14, f32[27,5,2304]{2,0,1:T(8,128)S(1)} %get-tuple-element.15, f32[27,5,2304]{2,0,1:T(8,128)S(1)} %get-tuple-element.16, ...), kind=kLoop, calls=%fused_computation.91 | loop fusion | flops 28926720 | bytes 37897416 | tf_op jit(solution)/shard_map/convert_element_type | solution.py:87
  117.0 2.1 copy.14
  119.2 29.7 %all-gather.5.cloned.1.call-done = bf16[216,3,2304]{2,1,0:T(4,128)(2,1)} async-done(((bf16[27,3,2304]{2,1,0:T(4,128)(2,1)}), bf16[216,3,2304]{2,1,0:T(4,128)(2,1)}) %all-gather.5.cloned.1.call-update) | async-done | bytes 2986000 | tf_op jit(solution)/shard_map/all_gather | solution.py:74
  148.9 3.2 %convolution_convert_fusion = bf16[7,27,3,2304]{3,1,2,0:T(8,128)(2,1)S(1)} fusion(bf16[216,3,2304]{2,1,0:T(4,128)(2,1)} %all-gather.5.cloned.1.call-done, bf16[7,216,216]{2,1,0:T(8,128)(2,1)} %copy-done.4, s32[]{:T(128)S(6)} %select_n.521), kind=kOutput, calls=%fused_computation.5 | convolution fusion | flops 565657344 | bytes 6708740 | tf_op jit(solution)/shard_map/krc,cpv->krpv/dot_general | solution.py:71
  152.8 4.7 %collective-permute-start.5 = (bf16[7,27,1,2304]{3,0,2,1:T(8,128)(2,1)S(1)}, bf16[7,27,1,2304]{3,0,2,1:T(8,128)(2,1)S(1)}, u32[]{:S(2)}, u32[]{:S(2)}) collective-permute-start(bf16[7,27,1,2304]{3,0,2,1:T(8,128)(2,1)S(1)} %copy.17), channel_id=1, source_target_pairs={{1,0},{2,1},{3,2},{4,3},{5,4},{6,5},{7,6},{8,7},{9,8},{10,9},{11,1... | collective-permute-start | bytes 2612744 | tf_op jit(solution)/shard_map/ppermute | solution.py:20
  158.0 2.1 collective-permute-start.4
  160.1 18.4 %collective-permute-done.5 = bf16[7,27,1,2304]{3,0,2,1:T(8,128)(2,1)S(1)} collective-permute-done((bf16[7,27,1,2304]{3,0,2,1:T(8,128)(2,1)S(1)}, bf16[7,27,1,2304]{3,0,2,1:T(8,128)(2,1)S(1)}, u32[]{:S(2)}, u32[]{:S(2)}) %collective-permute-start.5) | collective-permute-done | bytes 870944 | tf_op jit(solution)/shard_map/ppermute | solution.py:20
  178.7 6.3 %collective-permute-done.4 = bf16[7,27,1,2304]{3,0,2,1:T(8,128)(2,1)S(1)} collective-permute-done((bf16[7,27,1,2304]{3,0,2,1:T(8,128)(2,1)S(1)}, bf16[7,27,1,2304]{3,0,2,1:T(8,128)(2,1)S(1)}, u32[]{:S(2)}, u32[]{:S(2)}) %collective-permute-start.4) | collective-permute-done | bytes 870944 | tf_op jit(solution)/shard_map/ppermute | solution.py:17
  196.4 1.6 fusion.183
  201.0 12.3 %fusion.12 = bf16[27,3,2304]{2,0,1:T(8,128)(2,1)} fusion(f32[27,5,2304]{2,0,1:T(8,128)S(1)} %get-tuple-element.5, f32[27,5,2304]{2,0,1:T(8,128)S(1)} %get-tuple-element.6, f32[27,5,2304]{2,0,1:T(8,128)S(1)} %get-tuple-element.7, f32[27,5,2304]{2,0,1:T(8,128)S(1)} %get-tuple-element.8, f32[27,5,2304]{2,0,1:T(8,128)S(1)} %get-tuple-element.9, ...), kind=kLoop, calls=%fused_computation.20 | loop fusion | flops 28926720 | bytes 37897416 | tf_op jit(solution)/shard_map/convert_element_type | solution.py:87
  (88 shorter events, 39.1 us)
Async XLA Ops:
  7.2 10.6 %copy-start = (s32[210]{0:T(256)S(1)}, s32[210]{0:T(256)}, u32[]{:S(2)}) copy-start(s32[210]{0:T(256)} %param.11) | copy-start | bytes 2524
  7.2 10.3 %copy-start.3 = (f32[3,2304]{1,0:T(4,128)S(1)}, f32[3,2304]{1,0:T(4,128)}, u32[]{:S(2)}) copy-start(f32[3,2304]{1,0:T(4,128)} %param.7) | copy-start | bytes 82948
  7.2 10.5 %copy-start.5 = (s32[1218,3]{0,1:T(4,128)S(1)}, s32[1218,3]{0,1:T(4,128)}, u32[]{:S(2)}) copy-start(s32[1218,3]{0,1:T(4,128)} %param.10) | copy-start | bytes 43852
  7.2 45.4 %all-gather.3.cloned.1.call-start = ((), (), s32[]{:S(2)}) async-start(), calls=%async_computation | async-start | bytes 4478976 | tf_op jit(solution)/shard_map/all_gather | solution.py:74
  8.5 36.0 %collective-permute-start = (f32[7,1,2304]{2,1,0:T(1,128)S(1)}, f32[7,1,2304]{2,1,0:T(1,128)S(1)}, u32[]{:S(2)}, u32[]{:S(2)}) collective-permute-start(f32[7,1,2304]{2,1,0:T(1,128)S(1)} %get-tuple-element.94), channel_id=1, source_target_pairs={{1,0},{2,1},{3,2},{4,3},{5,4},{6,5},{7,6},{8,7},{9,8},{10,9},{11,1... | collective-permute-start | bytes 193544 | tf_op jit(solution)/shard_map/ppermute | solution.py:20
  13.4 31.1 %collective-permute-start.3 = (f32[7,1,2304]{2,1,0:T(1,128)S(1)}, f32[7,1,2304]{2,1,0:T(1,128)S(1)}, u32[]{:S(2)}, u32[]{:S(2)}) collective-permute-start(f32[7,1,2304]{2,1,0:T(1,128)S(1)} %get-tuple-element.95), channel_id=1, source_target_pairs={{0,1},{1,2},{2,3},{3,4},{4,5},{5,6},{6,7},{7,8},{8,9},{9,10},{10,1... | collective-permute-start | bytes 193544 | tf_op jit(solution)/shard_map/ppermute | solution.py:17
  17.4 131.4 %all-gather.5.cloned.1.call-start = ((), (), s32[]{:S(2)}) async-start(), calls=%async_computation.1 | async-start | bytes 4478976 | tf_op jit(solution)/shard_map/all_gather | solution.py:74
  25.8 8.0 %copy-start.7 = (s32[3]{0:T(128)S(1)}, s32[3]{0:T(128)}, u32[]{:S(2)}) copy-start(s32[3]{0:T(128)} %constant.254) | copy-start | bytes 40
  25.8 8.1 %copy-start.6 = (s32[3]{0:T(128)S(1)}, s32[3]{0:T(128)}, u32[]{:S(2)}) copy-start(s32[3]{0:T(128)} %constant.251) | copy-start | bytes 40
  41.8 2.7 %copy-start.2 = (f32[6,3,2304]{2,1,0:T(4,128)S(1)}, f32[6,3,2304]{2,1,0:T(4,128)}, u32[]{:S(2)}) copy-start(f32[6,3,2304]{2,1,0:T(4,128)} %param.8) | copy-start | bytes 497668
  44.4 8.2 %copy-start.4 = (bf16[7,216,216]{2,1,0:T(8,128)(2,1)}, bf16[7,216,216]{2,1,0:T(8,128)(2,1)S(1)}, u32[]{:S(2)}) copy-start(bf16[7,216,216]{2,1,0:T(8,128)(2,1)S(1)} %reshape.112) | copy-start | bytes 1959556
  57.0 25.7 %collective-permute-start.2 = (bf16[7,27,1,2304]{3,0,2,1:T(8,128)(2,1)S(1)}, bf16[7,27,1,2304]{3,0,2,1:T(8,128)(2,1)S(1)}, u32[]{:S(2)}, u32[]{:S(2)}) collective-permute-start(bf16[7,27,1,2304]{3,0,2,1:T(8,128)(2,1)S(1)} %copy.11), channel_id=1, source_target_pairs={{1,0},{2,1},{3,2},{4,3},{5,4},{6,5},{7,6},{8,7},{9,8},{10,9},{11,1... | collective-permute-start | bytes 2612744 | tf_op jit(solution)/shard_map/ppermute | solution.py:20
  61.6 27.0 %collective-permute-start.1 = (bf16[7,27,1,2304]{3,0,2,1:T(8,128)(2,1)S(1)}, bf16[7,27,1,2304]{3,0,2,1:T(8,128)(2,1)S(1)}, u32[]{:S(2)}, u32[]{:S(2)}) collective-permute-start(bf16[7,27,1,2304]{3,0,2,1:T(8,128)(2,1)S(1)} %copy.10), channel_id=1, source_target_pairs={{0,1},{1,2},{2,3},{3,4},{4,5},{5,6},{6,7},{7,8},{8,9},{9,10},{10,1... | collective-permute-start | bytes 2612744 | tf_op jit(solution)/shard_map/ppermute | solution.py:17
  152.8 25.7 %collective-permute-start.5 = (bf16[7,27,1,2304]{3,0,2,1:T(8,128)(2,1)S(1)}, bf16[7,27,1,2304]{3,0,2,1:T(8,128)(2,1)S(1)}, u32[]{:S(2)}, u32[]{:S(2)}) collective-permute-start(bf16[7,27,1,2304]{3,0,2,1:T(8,128)(2,1)S(1)} %copy.17), channel_id=1, source_target_pairs={{1,0},{2,1},{3,2},{4,3},{5,4},{6,5},{7,6},{8,7},{9,8},{10,9},{11,1... | collective-permute-start | bytes 2612744 | tf_op jit(solution)/shard_map/ppermute | solution.py:20
  158.0 27.0 %collective-permute-start.4 = (bf16[7,27,1,2304]{3,0,2,1:T(8,128)(2,1)S(1)}, bf16[7,27,1,2304]{3,0,2,1:T(8,128)(2,1)S(1)}, u32[]{:S(2)}, u32[]{:S(2)}) collective-permute-start(bf16[7,27,1,2304]{3,0,2,1:T(8,128)(2,1)S(1)} %copy.16), channel_id=1, source_target_pairs={{0,1},{1,2},{2,3},{3,4},{4,5},{5,6},{6,7},{7,8},{8,9},{9,10},{10,1... | collective-permute-start | bytes 2612744 | tf_op jit(solution)/shard_map/ppermute | solution.py:17
  201.0 12.3 %copy-start.1 = (s32[210]{0:T(256)S(1)}, s32[210]{0:T(256)}, u32[]{:S(2)}) copy-start(s32[210]{0:T(256)} %param.11) | copy-start | bytes 2524
Sparse Core Ops, SparseCore 0:
  17.6 35.0 all-gather.2
  119.3 29.5 all-gather.4
where the time goes:
time: 221 us; the launch traced here: 220 us
  waiting for transfers between devices  81.6 us (37%)
  local copies, waits for them, and re-layouts  54.2 us (25%)
  other arithmetic  43 us (19%)
  starting transfers between devices  20.5 us (9%)
  between operations  14.5 us (7%)
  matrix products  6.38 us (3%)
    ppermute x3, waiting for transfers between devices, padded(): lax.ppermute(lax.slice_in_dim(block, 0, width, axis=dim), axis, backward)  36.4 us
    all_gather x2, waiting for transfers between devices, combine(): lax.all_gather(own_panels, 'chaos', axis=0, tiled=True)  33.1 us
    slice x36, local copies, waits for them, and re-layouts, shifted(): moved_values = jnp.pad(source[..., offset:], padding + [(0, offset)])  28.5 us
    convert_element_type x2, other arithmetic, galerkin_apply(): return (scale_factor * result).astype(jnp.bfloat16)  24.6 us
    ppermute x3, starting transfers between devices, padded(): lax.ppermute(lax.slice_in_dim(block, 0, width, axis=dim), axis, backward)  14.2 us
    ppermute x3, waiting for transfers between devices, padded(): lax.ppermute(lax.slice_in_dim(block, block.shape[dim] - width, None, axis...  12.1 us
    gather x1, local copies, waits for them, and re-layouts, shards(): column_slot = owner_slot[triples[:, 1]]  7.98 us
    gather x1, local copies, waits for them, and re-layouts, shards(): row_slot = owner_slot[triples[:, 0]]  7.98 us
  transfers between devices with their start and end apart: 8, of which 6 were waited for; matrix products, arithmetic and copies ran while one was open for 16% of the time, Pallas kernels for 0%

commit v1 on v0

v1 whole, which is shorter than its diff:
```python
import functools

import jax
import jax.numpy as jnp
from jax import lax
from jax.experimental import pallas as pl
from jax.experimental.pallas import tpu as pltpu
from jax.sharding import PartitionSpec as P

MESH = pl.DeviceIdType.MESH
SIDE = 48
CELLS = 288
WIN = 384
PAD = 32
HALF = 0.5 * 0.15


def tile_window(part):
    start = CELLS * part - SIDE
    return start // 128, start % 128


def kernel(
    groups, slabs, fields, nnz,
    panel_ref, coef_ref, row_ref, col_ref, val_ref,
    first_ref, second_ref,
    send_buf, x1, x2, y1, y2, halo_low, halo_high, land1, land2,
    coef_low, coef_high, weight, onehot_rows, onehot_cols, table, scaled,
    a2a_send, a2a_recv, self_sem, z_send, z_recv, c_send, c_recv,
    h_send, h_recv, o1_send, o1_recv, o2_send, o2_recv, z2_send, z2_recv,
):
    part = lax.axis_index("chaos")
    slab = lax.axis_index("space")
    own_rows = panel_ref.shape[1]
    has_low, has_high = slab > 0, slab < slabs - 1
    left, right = part > 0, part < groups - 1
    bf16, f32 = jnp.bfloat16, jnp.float32

    barrier = pltpu.get_barrier_semaphore()
    for step in range(1, groups):
        peer = lax.rem(part + step, groups)
        pl.semaphore_signal(barrier, inc=1, device_id=(peer, slab), device_id_type=MESH)

    @pl.when(has_low)
    def _():
        pl.semaphore_signal(barrier, inc=1, device_id=(part, slab - 1), device_id_type=MESH)

    @pl.when(has_high)
    def _():
        pl.semaphore_signal(barrier, inc=1, device_id=(part, slab + 1), device_id_type=MESH)

    lane = lax.broadcasted_iota(jnp.int32, (1, WIN), 1)
    send_buf[...] = jnp.zeros_like(send_buf)
    for target in range(groups):
        tile, offset = tile_window(target)
        first, last = max(tile, 0), min(tile + 4, 18)
        for plane in range(3):
            block = panel_ref[plane, :, first * 128 : last * 128].astype(f32)
            if tile < 0:
                block = jnp.where(lane >= SIDE, pltpu.roll(block, SIDE, 1), 0.0)
            elif last - first == 3:
                block = jnp.where(lane < WIN - SIDE, pltpu.roll(block, WIN - offset, 1), 0.0)
            else:
                block = pltpu.roll(block, 512 - offset, 1)[:, :WIN]
            send_buf[target, plane, 0:own_rows, :] = block.astype(bf16)

    pl.semaphore_wait(barrier, groups - 1 + has_low.astype(jnp.int32) + has_high.astype(jnp.int32))

    def rows_of(group):
        return pl.ds(pl.multiple_of(group * PAD, PAD), PAD)

    def a2a(peer, source):
        return pltpu.make_async_remote_copy(
            src_ref=send_buf.at[peer],
            dst_ref=x1.at[pl.ds(1, 3), rows_of(source), :],
            send_sem=a2a_send.at[peer],
            recv_sem=a2a_recv.at[source],
            device_id=(peer, slab),
            device_id_type=MESH,
        )

    for step in range(1, groups):
        a2a(lax.rem(part + step, groups), part).start()
    own = pltpu.make_async_copy(send_buf.at[part], x1.at[pl.ds(1, 3), rows_of(part), :], self_sem)
    own.start()

    def to_slab(source, target, sems, index, other):
        return pltpu.make_async_remote_copy(
            src_ref=source, dst_ref=target, send_sem=sems[0].at[index], recv_sem=sems[1].at[index],
            device_id=(part, other), device_id_type=MESH,
        )

    def low_copy(source, target, sems):
        return to_slab(source, target, sems, 0, slab - 1)

    def high_copy(source, target, sems):
        return to_slab(source, target, sems, 1, slab + 1)

    c_sems, z_sems, z2_sems = (c_send, c_recv), (z_send, z_recv), (z2_send, z2_recv)

    def start_planes(low, high):
        pl.when(has_low)(lambda: low().start())
        pl.when(has_high)(lambda: high().start())

    def finish_planes(low, high):
        @pl.when(has_low)
        def _():
            low().wait_send()
            high().wait_recv()

        @pl.when(has_high)
        def _():
            high().wait_send()
            low().wait_recv()

    @pl.when(jnp.logical_not(has_low))
    def _():
        coef_low[...] = jnp.zeros_like(coef_low)

    @pl.when(jnp.logical_not(has_high))
    def _():
        coef_high[...] = jnp.zeros_like(coef_high)

    return_low = lambda: low_copy(coef_ref.at[0], coef_high, c_sems)
    return_high = lambda: high_copy(coef_ref.at[2], coef_low, c_sems)
    start_planes(return_low, return_high)

    entries = row_ref.shape[1]
    value = val_ref[...]
    top = value.astype(bf16).astype(f32)
    middle = (value - top).astype(bf16).astype(f32)
    bottom = value - top - middle

    @pl.loop(0, 16)
    def _(block):
        index = lax.broadcasted_iota(jnp.int32, (16, entries), 0) + block * 16
        hit = row_ref[...] == index
        for piece, part_value in enumerate((top, middle, bottom)):
            at = pl.ds(pl.multiple_of(piece * 256 + block * 16, 16), 16)
            onehot_rows[at, :] = jnp.where(hit, part_value, 0.0).astype(bf16)

    @pl.loop(0, fields)
    def _(field):
        @pl.loop(0, 16)
        def _(block):
            index = lax.broadcasted_iota(jnp.int32, (16, entries), 0) + (field * 256 + block * 16)
            at = pl.ds(pl.multiple_of(block * 16, 16), 16)
            onehot_cols[at, :] = jnp.where(col_ref[...] == index, 1.0, 0.0).astype(bf16)

        pieces = lax.dot_general(
            onehot_rows[...], onehot_cols[...], (((1,), (1,)), ((), ())), preferred_element_type=f32
        )
        table[:, pl.ds(pl.multiple_of(field * 256, 256), 256)] = (
            pieces[0:256] + pieces[256:512] + pieces[512:768]
        ).astype(bf16)

    finish_planes(return_low, return_high)

    cell = lax.rem(lane, SIDE)
    inside_up, inside_down = cell < SIDE - 1, cell > 0
    for plane in range(3):
        here = coef_ref[plane]
        below = coef_low[...] if plane == 0 else coef_ref[plane - 1]
        above = coef_high[...] if plane == 2 else coef_ref[plane + 1]
        sides = (
            jnp.where(inside_up, pltpu.roll(here, WIN - 1, 1), 0.0),
            jnp.where(inside_down, pltpu.roll(here, 1, 1), 0.0),
            pltpu.roll(here, WIN - SIDE, 1),
            pltpu.roll(here, SIDE, 1),
            above,
            below,
        )
        for face, side in enumerate(sides):
            half = HALF * (here + side)
            for field in range(fields):
                weight[plane, field, face] = jnp.broadcast_to(half[field : field + 1], (8, WIN))

    def apply(x, y):
        @pl.loop(0, 3)
        def _(plane):
            @pl.loop(0, 16)
            def _(block):
                at = pl.ds(pl.multiple_of(block * 16, 16), 16)
                here = x[plane + 1, at, :].astype(f32)
                sides = (
                    jnp.where(inside_up, pltpu.roll(here, WIN - 1, 1), 0.0),
                    jnp.where(inside_down, pltpu.roll(here, 1, 1), 0.0),
                    pltpu.roll(here, WIN - SIDE, 1),
                    pltpu.roll(here, SIDE, 1),
                    x[plane + 2, at, :].astype(f32),
                    x[plane, at, :].astype(f32),
                )
                drops = [(here - side).reshape(2, 8, WIN) for side in sides]
                for field in range(fields):
                    flux = weight[plane, field, 0] * drops[0]
                    for face in range(1, 6):
                        flux = flux + weight[plane, field, face] * drops[face]
                    to = pl.ds(pl.multiple_of(field * 256 + block * 16, 16), 16)
                    scaled[to, :] = flux.reshape(16, WIN).astype(bf16)

            y[plane] = jnp.dot(table[...], scaled[...], preferred_element_type=f32).astype(bf16)

    for group in range(groups):
        @pl.when(group != part)
        def _():
            a2a(group, part).wait_send()
            a2a(part, group).wait_recv()
    own.wait()

    def clear_ends(x):
        @pl.when(jnp.logical_not(has_low))
        def _():
            x[0] = jnp.zeros(x.shape[1:], x.dtype)

        @pl.when(jnp.logical_not(has_high))
        def _():
            x[4] = jnp.zeros(x.shape[1:], x.dtype)

    clear_ends(x1)
    planes_low = lambda: low_copy(x1.at[1], x1.at[4], z_sems)
    planes_high = lambda: high_copy(x1.at[3], x1.at[0], z_sems)
    start_planes(planes_low, planes_high)
    finish_planes(planes_low, planes_high)

    apply(x1, y1)

    clear_ends(x2)
    next_low = lambda: low_copy(y1.at[0], x2.at[4], z2_sems)
    next_high = lambda: high_copy(y1.at[2], x2.at[0], z2_sems)
    start_planes(next_low, next_high)

    def row_copy(lanes, target, index, other):
        return pltpu.make_async_remote_copy(
            src_ref=y1.at[:, :, lanes], dst_ref=target, send_sem=h_send.at[index],
            recv_sem=h_recv.at[index], device_id=(other, slab), device_id_type=MESH,
        )

    rows_left = lambda: row_copy(pl.ds(0, 128), halo_high, 0, part - 1)
    rows_right = lambda: row_copy(pl.ds(256, 128), halo_low, 1, part + 1)
    pl.when(left)(lambda: rows_left().start())
    pl.when(right)(lambda: rows_right().start())

    def out_copy(y, land, peer, source, sems):
        return pltpu.make_async_remote_copy(
            src_ref=y.at[:, rows_of(peer), :], dst_ref=land.at[source],
            send_sem=sems[0].at[peer], recv_sem=sems[1].at[source],
            device_id=(peer, slab), device_id_type=MESH,
        )

    def start_out(y, land, sems):
        for step in range(1, groups):
            out_copy(y, land, lax.rem(part + step, groups), part, sems).start()

    def finish_out(y, land, sems):
        for group in range(groups):
            @pl.when(group != part)
            def _():
                out_copy(y, land, group, part, sems).wait_send()
                out_copy(y, land, part, group, sems).wait_recv()

    o1_sems, o2_sems = (o1_send, o1_recv), (o2_send, o2_recv)
    start_out(y1, land1, o1_sems)
    own1 = pltpu.make_async_copy(y1.at[:, rows_of(part), :], land1.at[part], self_sem)
    own1.start()

    @pl.when(left)
    def _():
        rows_left().wait_send()
        rows_right().wait_recv()

    @pl.when(right)
    def _():
        rows_right().wait_send()
        rows_left().wait_recv()

    @pl.when(jnp.logical_not(left))
    def _():
        halo_low[...] = jnp.zeros_like(halo_low)

    @pl.when(jnp.logical_not(right))
    def _():
        halo_high[...] = jnp.zeros_like(halo_high)

    tile_lane = lax.broadcasted_iota(jnp.int32, (1, 128), 1)

    @pl.loop(0, 3)
    def _(plane):
        @pl.loop(0, 8)
        def _(block):
            at = pl.ds(pl.multiple_of(block * 32, 32), 32)
            low = pltpu.roll(halo_low[plane, at, :].astype(f32), 96, 1)
            high = pltpu.roll(halo_high[plane, at, :].astype(f32), 32, 1)
            x2[plane + 1, at, 0:128] = jnp.where(
                tile_lane < 48, low, y1[plane, at, 0:128].astype(f32)
            ).astype(bf16)
            x2[plane + 1, at, 128:256] = y1[plane, at, 128:256]
            x2[plane + 1, at, 256:384] = jnp.where(
                tile_lane >= 80, high, y1[plane, at, 256:384].astype(f32)
            ).astype(bf16)

    finish_planes(next_low, next_high)
    apply(x2, y2)

    start_out(y2, land2, o2_sems)
    own1.wait()
    own2 = pltpu.make_async_copy(y2.at[:, rows_of(part), :], land2.at[part], self_sem)
    own2.start()

    def assemble(land, out_ref):
        for plane in range(3):
            carry = None
            for source in range(groups):
                tile, offset = divmod(CELLS * source, 128)
                block = land[source, plane, 0:own_rows, :].astype(f32)
                block = pltpu.roll(block, (offset - SIDE) % WIN, 1)
                head = block[:, 0:128]
                if offset:
                    head = jnp.where(tile_lane < offset, carry, head)
                out_ref[plane, :, tile * 128 : tile * 128 + 128] = head.astype(bf16)
                out_ref[plane, :, tile * 128 + 128 : tile * 128 + 256] = block[:, 128:256].astype(bf16)
                carry = block[:, 256:384]
                if offset + CELLS == WIN:
                    out_ref[plane, :, tile * 128 + 256 : tile * 128 + 384] = carry.astype(bf16)

    finish_out(y1, land1, o1_sems)
    assemble(land1, first_ref)
    own2.wait()
    finish_out(y2, land2, o2_sems)
    assemble(land2, second_ref)


def shards(groups, slabs, panels, mean_field, fluctuations, products, triples, owner_slot):
    own_rows, planes, plane_cells = panels.shape
    fields, nnz = 1 + fluctuations.shape[0], products.shape[0]
    entries = -(-nnz // 128) * 128
    part = lax.axis_index("chaos")
    panel_planes = jnp.transpose(panels, (1, 0, 2))
    coef = jnp.concatenate([mean_field[None], fluctuations], axis=0)
    coef = jnp.pad(coef, ((0, 1), (0, 0), (SIDE, SIDE)))
    coef = lax.dynamic_slice_in_dim(coef, part * CELLS, WIN, axis=2)
    coef = jnp.transpose(coef, (1, 0, 2))
    padded_slot = owner_slot + (PAD - own_rows) * (owner_slot // own_rows)
    names = lax.iota(jnp.int32, owner_slot.shape[0])

    def slots(indices):
        return jnp.sum(jnp.where(indices[:, None] == names[None, :], padded_slot[None, :], 0), axis=1)

    row = jnp.pad(slots(triples[:, 0]), (0, entries - nnz))[None]
    col = jnp.pad(slots(triples[:, 1]) + 256 * triples[:, 2], (0, entries - nnz))[None]
    val = jnp.pad(products, (0, entries - nnz))[None]

    vmem = pl.BlockSpec(memory_space=pltpu.VMEM)
    out = jax.ShapeDtypeStruct(panel_planes.shape, jnp.bfloat16)
    bf16, f32 = jnp.bfloat16, jnp.float32
    dma = pltpu.SemaphoreType.DMA
    first, second = pl.pallas_call(
        functools.partial(kernel, groups, slabs, fields, nnz),
        out_shape=(out, out),
        in_specs=[vmem] * 5,
        out_specs=(vmem, vmem),
        scratch_shapes=[
            pltpu.VMEM((groups, 3, PAD, WIN), bf16),
            pltpu.VMEM((5, 256, WIN), bf16),
            pltpu.VMEM((5, 256, WIN), bf16),
            pltpu.VMEM((3, 256, WIN), bf16),
            pltpu.VMEM((3, 256, WIN), bf16),
            pltpu.VMEM((3, 256, 128), bf16),
            pltpu.VMEM((3, 256, 128), bf16),
            pltpu.VMEM((groups, 3, PAD, WIN), bf16),
            pltpu.VMEM((groups, 3, PAD, WIN), bf16),
            pltpu.VMEM((8, WIN), f32),
            pltpu.VMEM((8, WIN), f32),
            pltpu.VMEM((3, fields, 6, 8, WIN), f32),
            pltpu.VMEM((768, entries), bf16),
            pltpu.VMEM((256, entries), bf16),
            pltpu.VMEM((256, fields * 256), bf16),
            pltpu.VMEM((fields * 256, WIN), bf16),
            dma((groups,)), dma((groups,)), dma,
            dma((2,)), dma((2,)), dma((2,)), dma((2,)), dma((2,)), dma((2,)),
            dma((groups,)), dma((groups,)), dma((groups,)), dma((groups,)),
            dma((2,)), dma((2,)),
        ],
        compiler_params=pltpu.CompilerParams(
            collective_id=0, has_side_effects=True, vmem_limit_bytes=48 * 1024 * 1024
        ),
    )(panel_planes, coef, row, col, val)
    return jnp.transpose(first, (1, 0, 2)), jnp.transpose(second, (1, 0, 2))


def solution(mesh):
    in_specs = (P("chaos", "space", None), P("space", None), P(None, "space", None), P(), P(), P())
    out_specs = (P("chaos", "space", None), P("chaos", "space", None))
    body = functools.partial(shards, mesh.shape["chaos"], mesh.shape["space"])
    return jax.shard_map(body, mesh=mesh, in_specs=in_specs, out_specs=out_specs, check_vma=False)
```

time: 221 us -> 64.9 us (0.29)
  waiting for transfers between devices: 81.6 us -> 0 us
  Pallas kernels: 0 us -> 57.8 us
  local copies, waits for them, and re-layouts: 54.2 us -> 4.07 us
  other arithmetic: 43 us -> 2.05 us
  starting transfers between devices: 20.5 us -> 0 us
  between operations: 14.5 us -> 0.72 us
  matrix products: 6.38 us -> 0 us
    pallas_call x0 -> x1, Pallas kernels: none -> 57.8 us  [shards(): pl.pallas_call(functools.partial(kernel, groups, slabs, fields, nnz), out...]
    ppermute x6 -> x0, waiting for transfers between devices: 48.5 us -> none  [the longest x3 36.4 us: padded(): lax.ppermute(lax.slice_in_dim(block, 0, width, axis=dim), axis, backward)]
    all_gather x2 -> x0, waiting for transfers between devices: 33.1 us -> none  [combine(): lax.all_gather(own_panels, 'chaos', axis=0, tiled=True)]
    slice x42 -> x0, local copies, waits for them, and re-layouts: 30.8 us -> none  [the longest x36 28.5 us: shifted(): moved_values = jnp.pad(source[..., offset:], padding + [(0, offset)])]
    convert_element_type x5 -> x0, other arithmetic: 27.2 us -> none  [the longest x2 24.6 us: galerkin_apply(): return (scale_factor * result).astype(jnp.bfloat16)]
    ppermute x6 -> x0, starting transfers between devices: 20.4 us -> none  [the longest x3 14.2 us: padded(): lax.ppermute(lax.slice_in_dim(block, 0, width, axis=dim), axis, backward)]
    gather x2 -> x0, local copies, waits for them, and re-layouts: 16 us -> none  [the longest x1 7.98 us: shards(): column_slot = owner_slot[triples[:, 1]]]
    unnamed x4 -> x0, other arithmetic: 7.96 us -> none
  transfers between devices with their start and end apart: 8 -> 0, of which waited for: 6 -> 0; matrix products, arithmetic and copies ran while one was open for 16% -> 0% of each run, Pallas kernels for 0% -> 0%
where the time goes in v1:
time: 64.9 us; the launch traced here: 64.6 us
  Pallas kernels  57.8 us (89%)
  local copies, waits for them, and re-layouts  4.07 us (6%)
  other arithmetic  2.05 us (3%)
  between operations  0.72 us (1%)
    pallas_call x1, Pallas kernels, shards(): pl.pallas_call(functools.partial(kernel, groups, slabs, fields, nnz), out...  57.8 us
    unnamed x5, local copies, waits for them, and re-layouts  2.51 us

profile of v1, /device:TPU:7, one launch (start us, length us, event | category | flops | bytes accessed | tf_op | source)
XLA Modules:
  0.0 64.6 jit_solution(14083926596970691736)
XLA Ops:
  0.6 0.7 %multiply_add_fusion = s32[210]{0:T(256)S(1)} fusion(s32[210]{0:T(256)} %param.11), kind=kLoop, calls=%fused_computation.22 | loop fusion | flops 2100 | bytes 1680 | tf_op jit(solution)/shard_map/add | solution.py:342
  1.3 0.7 %pad.18 = f32[1280]{0:T(1024)S(1)} pad(f32[1218]{0:T(1024)} %param.9, f32[]{:T(128)} %constant.7.clone.1), padding=0_62 | pad | bytes 9996 | tf_op jit(solution)/shard_map/jit(_pad)/pad | solution.py:350
  2.0 0.9 %multiply_reduce_fusion = (s32[1218]{0:T(1024)S(1)}, s32[1218]{0:T(1024)S(1)}, s32[1218]{0:T(1024)S(1)}) fusion(s32[1218,3]{0,1:T(4,128)} %param.10), kind=kLoop, calls=%fused_computation.18 | loop fusion | flops 1218 | bytes 29232 | tf_op jit(solution)/shard_map/mul | solution.py:349
  2.9 0.4 select_reduce_fusion
  3.3 0.0 copy-start
  3.4 0.8 %broadcast_in_dim.32 = f32[1,3,2304]{2,0,1:T(1,128)S(1)} reshape(f32[3,2304]{1,0:T(4,128)} %param.7) | data formatting | bytes 55296 | tf_op jit(solution)/shard_map/broadcast_in_dim | solution.py:338
  4.2 1.0 %copy.9 = f32[6,3,2304]{2,0,1:T(8,128)S(1)} copy(f32[6,3,2304]{2,1,0:T(4,128)} %param.8) | data formatting | bytes 331776 | tf_op args[2]
  5.2 0.1 fusion.3.coef_ref
  5.3 0.0 copy-done
  5.3 57.8 %shard_map.77 = (bf16[3,27,2304]{2,1,0:T(8,128)(2,1)S(1)}, bf16[3,27,2304]{2,1,0:T(8,128)(2,1)S(1)}) custom-call(bf16[3,27,2304]{2,1,0:T(8,128)(2,1)S(1)} %bitcast.7, f32[3,8,384]{2,1,0:T(8,128)S(1)} %fusion.3.coef_ref, s32[1,1280]{1,0:T(1,128)S(1)} %broadcast_in_dim.35.row_ref, s32[1,1280]{1,0:T(1,128)S(1)} %broadcast_in_dim.36.col_ref, ...), custom_call_target="tpu_custom_call" | custom-call | tf_op jit(solution)/shard_map/pallas_call | solution.py:356
  63.1 0.8 %copy.12 = bf16[27,3,2304]{2,0,1:T(8,128)(2,1)} copy(bf16[27,3,2304]{2,0,1:T(8,128)(2,1)S(1)} %bitcast.6) | data formatting | bytes 746496
  63.9 0.8 %copy.13 = bf16[27,3,2304]{2,0,1:T(8,128)(2,1)} copy(bf16[27,3,2304]{2,0,1:T(8,128)(2,1)S(1)} %bitcast.5) | data formatting | bytes 746496
  (6 shorter events, 0.0 us)
Async XLA Ops:
  3.3 2.0 %copy-start = (bf16[27,3,2304]{2,0,1:T(8,128)(2,1)S(1)}, bf16[27,3,2304]{2,0,1:T(8,128)(2,1)}, u32[]{:S(2)}) copy-start(bf16[27,3,2304]{2,0,1:T(8,128)(2,1)} %param.6) | copy-start | bytes 1119748

commit v2 on v0

v2 whole, which is shorter than its diff:
```python
import functools

import jax
import jax.numpy as jnp
from jax import lax
from jax.experimental import pallas as pl
from jax.experimental.pallas import tpu as pltpu
from jax.sharding import PartitionSpec as P

MESH = pl.DeviceIdType.MESH
SIDE = 48
CELLS = 288
WIN = 384
FLAT = 896
PAD = 32
ROWS = 256
HALF = 0.5 * 0.15
CALC = jnp.bfloat16

ORDER = ((0, 0), (0, 1), (2, 0), (2, 1), (1, 0), (1, 1), (3, 0), (3, 1))


def tile_window(part):
    start = CELLS * part - SIDE
    return start // 128, start % 128


def linear_window(ref, index, part, lane):
    tile, offset = tile_window(part)
    first, last = max(tile, 0), min(tile + 4, 18)
    block = ref[index + (slice(first * 128, last * 128),)].astype(jnp.float32)
    if tile < 0:
        return jnp.where(lane >= SIDE, pltpu.roll(block, SIDE, 1), 0.0)
    if last - first == 3:
        return jnp.where(lane < WIN - SIDE, pltpu.roll(block, WIN - offset, 1), 0.0)
    return pltpu.roll(block, 512 - offset, 1)[:, :WIN]


def flatten(planes, tile_lane):
    a, b, c = planes
    return jnp.concatenate(
        [
            a[:, 0:256],
            jnp.where(tile_lane < 32, a[:, 256:384], b[:, 0:128]),
            b[:, 128:256],
            jnp.where(tile_lane < 64, b[:, 256:384], c[:, 0:128]),
            c[:, 128:384],
        ],
        axis=1,
    )


def kernel(
    groups, slabs, fields, nnz,
    panel_ref, mean_ref, fluct_ref, triple_ref, product_ref, slot_ref,
    first_ref, second_ref,
    send_buf, x1, x2, y1, y2, edge_low, edge_high, halo_low, halo_high, land1, land2,
    coef, coef_low, coef_high, weight, drops, onehot_rows, onehot_cols, table, scaled,
    a2a_send, a2a_recv, self_sem, z_send, z_recv, c_send, c_recv,
    h_send, h_recv, o1_send, o1_recv, o2_send, o2_recv, z2_send, z2_recv,
):
    part = lax.axis_index("chaos")
    slab = lax.axis_index("space")
    own_rows = panel_ref.shape[1]
    has_low, has_high = slab > 0, slab < slabs - 1
    left, right = part > 0, part < groups - 1
    bf16, f32 = jnp.bfloat16, jnp.float32
    chip, core = part // 2, lax.rem(part, 2)

    def group_of(step):
        far, other = ORDER[step]
        return lax.rem(chip + far, groups // 2) * 2 + lax.rem(core + other, 2)

    barrier = pltpu.get_barrier_semaphore()
    for step in range(1, groups):
        pl.semaphore_signal(barrier, inc=1, device_id=(group_of(step), slab), device_id_type=MESH)

    @pl.when(has_low)
    def _():
        pl.semaphore_signal(barrier, inc=1, device_id=(part, slab - 1), device_id_type=MESH)

    @pl.when(has_high)
    def _():
        pl.semaphore_signal(barrier, inc=1, device_id=(part, slab + 1), device_id_type=MESH)

    lane = lax.broadcasted_iota(jnp.int32, (1, WIN), 1)
    tile_lane = lax.broadcasted_iota(jnp.int32, (1, 128), 1)
    send_buf[:, :, 16:32, :] = jnp.zeros((groups, 3, 16, WIN), bf16)
    for target in range(groups):
        for plane in range(3):
            block = linear_window(panel_ref, (plane, slice(None)), target, lane)
            block = pltpu.roll(block, (32 * plane - SIDE) % WIN, 1)
            send_buf[target, plane, 0:own_rows, :] = block.astype(bf16)

    coef[...] = jnp.zeros_like(coef)
    for target in range(groups):
        @pl.when(part == target)
        def _():
            for plane in range(3):
                coef[plane, 0:1, :] = linear_window(mean_ref, (slice(plane, plane + 1),), target, lane)
                for field in range(1, fields):
                    coef[plane, field : field + 1, :] = linear_window(
                        fluct_ref, (field - 1, slice(plane, plane + 1)), target, lane
                    )

    pl.semaphore_wait(barrier, groups - 1 + has_low.astype(jnp.int32) + has_high.astype(jnp.int32))

    def rows_of(group):
        return pl.ds(pl.multiple_of(group * PAD, PAD), PAD)

    def a2a(peer, source):
        return pltpu.make_async_remote_copy(
            src_ref=send_buf.at[peer],
            dst_ref=x1.at[pl.ds(1, 3), rows_of(source), :],
            send_sem=a2a_send.at[peer],
            recv_sem=a2a_recv.at[source],
            device_id=(peer, slab),
            device_id_type=MESH,
        )

    own = pltpu.make_async_copy(send_buf.at[part], x1.at[pl.ds(1, 3), rows_of(part), :], self_sem)
    own.start()
    for step in (2, 3, 4, 5, 6, 7, 1):
        a2a(group_of(step), part).start()

    def to_slab(source, target, sems, index, other):
        return pltpu.make_async_remote_copy(
            src_ref=source, dst_ref=target, send_sem=sems[0].at[index], recv_sem=sems[1].at[index],
            device_id=(part, other), device_id_type=MESH,
        )

    def start_planes(low, high):
        pl.when(has_low)(lambda: low().start())
        pl.when(has_high)(lambda: high().start())

    def arrive_planes(low, high):
        pl.when(has_low)(lambda: high().wait_recv())
        pl.when(has_high)(lambda: low().wait_recv())

    def leave_planes(low, high):
        pl.when(has_low)(lambda: low().wait_send())
        pl.when(has_high)(lambda: high().wait_send())

    @pl.when(jnp.logical_not(has_low))
    def _():
        coef_low[...] = jnp.zeros_like(coef_low)
        x1[0] = jnp.zeros(x1.shape[1:], x1.dtype)
        x2[0] = jnp.zeros(x2.shape[1:], x2.dtype)

    @pl.when(jnp.logical_not(has_high))
    def _():
        coef_high[...] = jnp.zeros_like(coef_high)
        x1[4] = jnp.zeros(x1.shape[1:], x1.dtype)
        x2[4] = jnp.zeros(x2.shape[1:], x2.dtype)

    @pl.when(jnp.logical_not(left))
    def _():
        halo_low[...] = jnp.zeros_like(halo_low)

    @pl.when(jnp.logical_not(right))
    def _():
        halo_high[...] = jnp.zeros_like(halo_high)

    c_sems, z_sems, z2_sems = (c_send, c_recv), (z_send, z_recv), (z2_send, z2_recv)
    coef_copies = (
        lambda: to_slab(coef.at[0], coef_high, c_sems, 0, slab - 1),
        lambda: to_slab(coef.at[2], coef_low, c_sems, 1, slab + 1),
    )
    start_planes(*coef_copies)

    def x_planes(group):
        rows = rows_of(group)
        return (
            lambda: to_slab(x1.at[1, rows, :], x1.at[4, rows, :], z_sems, group, slab - 1),
            lambda: to_slab(x1.at[3, rows, :], x1.at[0, rows, :], z_sems, groups + group, slab + 1),
        )

    def y_planes(group):
        rows = rows_of(group)
        return (
            lambda: to_slab(y1.at[rows, pl.ds(0, WIN)], x2.at[4, rows, :], z2_sems, group, slab - 1),
            lambda: to_slab(
                y1.at[rows, pl.ds(FLAT - WIN, WIN)], x2.at[0, rows, :], z2_sems, groups + group, slab + 1
            ),
        )

    own.wait()
    start_planes(*x_planes(part))

    slot = slot_ref[...]
    slot = slot + (PAD - own_rows) * (slot // own_rows)
    name = lax.broadcasted_iota(jnp.int32, slot.shape, 0)

    def slots(index):
        hit = name == triple_ref[index : index + 1, :]
        return jnp.sum(jnp.where(hit, slot, 0), axis=0, keepdims=True)

    row = slots(0)
    column = slots(1) + ROWS * triple_ref[2:3, :]
    value = product_ref[...]
    top = value.astype(bf16).astype(f32)
    middle = (value - top).astype(bf16).astype(f32)
    bottom = value - top - middle
    last_tile = slice(nnz // 128 * 128, nnz // 128 * 128 + 128)
    onehot_rows[:, last_tile] = jnp.zeros((3 * ROWS, 128), bf16)
    onehot_cols[:, last_tile] = jnp.zeros((ROWS, 128), bf16)

    @pl.loop(0, 16)
    def _(block):
        hit = row == lax.broadcasted_iota(jnp.int32, (16, nnz), 0) + block * 16
        for piece, part_value in enumerate((top, middle, bottom)):
            at = pl.ds(pl.multiple_of(piece * ROWS + block * 16, 16), 16)
            onehot_rows[at, 0:nnz] = jnp.where(hit, part_value, 0.0).astype(bf16)

    @pl.loop(0, fields)
    def _(field):
        @pl.loop(0, 16)
        def _(block):
            index = lax.broadcasted_iota(jnp.int32, (16, nnz), 0) + (field * ROWS + block * 16)
            at = pl.ds(pl.multiple_of(block * 16, 16), 16)
            onehot_cols[at, 0:nnz] = jnp.where(column == index, 1.0, 0.0).astype(bf16)

        pieces = lax.dot_general(
            onehot_rows[...], onehot_cols[...], (((1,), (1,)), ((), ())), preferred_element_type=f32
        )
        table[:, pl.ds(pl.multiple_of(field * ROWS, ROWS), ROWS)] = (
            pieces[0:256] + pieces[256:512] + pieces[512:768]
        ).astype(bf16)

    arrive_planes(*coef_copies)
    inside = []
    for plane in range(3):
        cell = lax.rem(lane + (WIN - 32 * plane), SIDE)
        inside.append((cell < SIDE - 1, cell > 0))

    def neighbours(here, plane, above, below):
        up, down = inside[plane]
        return (
            jnp.where(up, pltpu.roll(here, WIN - 1, 1), 0.0),
            jnp.where(down, pltpu.roll(here, 1, 1), 0.0),
            pltpu.roll(here, WIN - SIDE, 1),
            pltpu.roll(here, SIDE, 1),
            above,
            below,
        )

    halves = []
    for plane in range(3):
        turn = lambda block: pltpu.roll(block, (32 * plane - SIDE) % WIN, 1)
        here = turn(coef[plane])
        below = turn(coef_low[...] if plane == 0 else coef[plane - 1])
        above = turn(coef_high[...] if plane == 2 else coef[plane + 1])
        halves.append([HALF * (here + side) for side in neighbours(here, plane, above, below)])
    for face in range(6):
        half = flatten([halves[plane][face] for plane in range(3)], tile_lane)
        for field in range(fields):
            weight[field, face] = jnp.broadcast_to(half[field : field + 1], (16, FLAT)).astype(CALC)

    def scale(x, start):
        at = pl.ds(pl.multiple_of(start, 16), 16)
        own_planes = [x[plane + 1, at, :].astype(f32) for plane in range(3)]
        faces = []
        for plane in range(3):
            here = own_planes[plane]
            if plane == 2:
                above = pltpu.roll(x[4, at, :].astype(f32), 64, 1)
            else:
                above = pltpu.roll(own_planes[plane + 1], WIN - 32, 1)
            if plane == 0:
                below = pltpu.roll(x[0, at, :].astype(f32), WIN - 64, 1)
            else:
                below = pltpu.roll(own_planes[plane - 1], 32, 1)
            faces.append([here - side for side in neighbours(here, plane, above, below)])
        for face in range(6):
            drops[face] = flatten([faces[plane][face] for plane in range(3)], tile_lane).astype(CALC)
        for first in range(0, FLAT, 256):
            lanes = slice(first, min(first + 256, FLAT))
            drop = [drops[face, :, lanes] for face in range(6)]
            for field in range(fields):
                terms = [weight[field, face, :, lanes] * drop[face] for face in range(6)]
                flux = (terms[0] + terms[1]) + (terms[2] + terms[3]) + (terms[4] + terms[5])
                to = pl.ds(pl.multiple_of(field * ROWS + start, 16), 16)
                scaled[to, lanes] = flux.astype(bf16)

    def scale_group(x, group):
        @pl.loop(0, PAD // 16)
        def _(block):
            scale(x, group * PAD + block * 16)

    def combine(y):
        for first in range(0, FLAT, 256):
            lanes = slice(first, min(first + 256, FLAT))
            y[:, lanes] = jnp.dot(table[...], scaled[:, lanes], preferred_element_type=f32).astype(bf16)

    for step in range(1, groups):
        group = group_of(step)
        a2a(part, group).wait_recv()
        start_planes(*x_planes(group))
    for step in range(groups):
        group = group_of(step)
        arrive_planes(*x_planes(group))
        scale_group(x1, group)
    combine(y1)

    for step in range(groups):
        start_planes(*y_planes(group_of(step)))

    @pl.loop(0, 16)
    def _(block):
        at = pl.ds(pl.multiple_of(block * 16, 16), 16)
        tile = [y1[at, t * 128 : t * 128 + 128].astype(f32) for t in range(7)]
        up = [pltpu.roll(tile[t], 32, 1) for t in (0, 4, 2)]
        edge_high[at, 0:128] = jnp.where((tile_lane >= 32) & (tile_lane < 80), up[0], up[1]).astype(bf16)
        edge_high[at, 128:256] = up[2].astype(bf16)
        down = [pltpu.roll(tile[t], 96, 1) for t in (1, 2, 6, 4)]
        edge_low[at, 0:128] = jnp.where(
            tile_lane >= 96, down[1], jnp.where(tile_lane >= 80, down[0], down[2])
        ).astype(bf16)
        edge_low[at, 128:256] = down[3].astype(bf16)

    def row_copy(source, target, index, other):
        return pltpu.make_async_remote_copy(
            src_ref=source, dst_ref=target, send_sem=h_send.at[index],
            recv_sem=h_recv.at[index], device_id=(other, slab), device_id_type=MESH,
        )

    rows_left = lambda: row_copy(edge_high, halo_high, 0, part - 1)
    rows_right = lambda: row_copy(edge_low, halo_low, 1, part + 1)
    pl.when(left)(lambda: rows_left().start())
    pl.when(right)(lambda: rows_right().start())

    def out_copy(y, land, peer, source, sems):
        return pltpu.make_async_remote_copy(
            src_ref=y.at[rows_of(peer), :], dst_ref=land.at[source],
            send_sem=sems[0].at[peer], recv_sem=sems[1].at[source],
            device_id=(peer, slab), device_id_type=MESH,
        )

    def start_out(y, land, sems):
        for step in (2, 3, 4, 5, 6, 7, 1):
            out_copy(y, land, group_of(step), part, sems).start()

    def leave_out(y, land, sems):
        for step in range(1, groups):
            out_copy(y, land, group_of(step), part, sems).wait_send()

    def arrive_out(y, land, sems):
        for step in range(1, groups):
            out_copy(y, land, part, group_of(step), sems).wait_recv()

    o1_sems, o2_sems = (o1_send, o1_recv), (o2_send, o2_recv)
    start_out(y1, land1, o1_sems)
    own1 = pltpu.make_async_copy(y1.at[rows_of(part), :], land1.at[part], self_sem)
    own1.start()

    pl.when(left)(lambda: rows_right().wait_recv())
    pl.when(right)(lambda: rows_left().wait_recv())

    @pl.loop(0, 16)
    def _(block):
        at = pl.ds(pl.multiple_of(block * 16, 16), 16)
        tile = [y1[at, t * 128 : t * 128 + 128].astype(f32) for t in (2, 4, 6)]
        high, high_b = (halo_high[at, t : t + 128].astype(f32) for t in (0, 128))
        low, low_b = (halo_low[at, t : t + 128].astype(f32) for t in (0, 128))
        x2[1, at, 0:256] = y1[at, 0:256]
        x2[1, at, 256:384] = jnp.where(
            tile_lane < 32, tile[0], jnp.where(tile_lane < 80, high, low)
        ).astype(bf16)
        x2[2, at, 0:128] = jnp.where(tile_lane < 32, low_b, tile[0]).astype(bf16)
        x2[2, at, 128:256] = y1[at, 384:512]
        x2[2, at, 256:384] = jnp.where(
            tile_lane < 64, tile[1], jnp.where(tile_lane < 112, high_b, low_b)
        ).astype(bf16)
        x2[3, at, 0:128] = jnp.where(
            tile_lane < 16, high, jnp.where(tile_lane < 64, low, tile[1])
        ).astype(bf16)
        x2[3, at, 128:256] = y1[at, 640:768]
        x2[3, at, 256:384] = jnp.where(tile_lane < 96, tile[2], high).astype(bf16)

    for step in range(groups):
        group = group_of(step)
        arrive_planes(*y_planes(group))
        scale_group(x2, group)
    combine(y2)
    start_out(y2, land2, o2_sems)
    own1.wait()
    own2 = pltpu.make_async_copy(y2.at[rows_of(part), :], land2.at[part], self_sem)
    own2.start()

    def assemble(land, out_ref):
        for plane in range(3):
            carry = None
            for source in range(groups):
                tile, offset = divmod(CELLS * source, 128)
                start = 256 * plane
                block = land[source, 0:own_rows, start : start + WIN].astype(f32)
                if offset != 32 * plane:
                    block = pltpu.roll(block, (offset - 32 * plane) % WIN, 1)
                head = block[:, 0:128]
                if offset:
                    head = jnp.where(tile_lane < offset, carry, head)
                out_ref[plane, :, tile * 128 : tile * 128 + 128] = head.astype(bf16)
                out_ref[plane, :, tile * 128 + 128 : tile * 128 + 256] = block[:, 128:256].astype(bf16)
                carry = block[:, 256:384]
                if offset + CELLS == WIN:
                    out_ref[plane, :, tile * 128 + 256 : tile * 128 + 384] = carry.astype(bf16)

    arrive_out(y1, land1, o1_sems)
    assemble(land1, first_ref)

    leave_planes(*coef_copies)
    for step in range(groups):
        leave_planes(*x_planes(group_of(step)))
        leave_planes(*y_planes(group_of(step)))
    for step in range(1, groups):
        a2a(group_of(step), part).wait_send()
    pl.when(left)(lambda: rows_left().wait_send())
    pl.when(right)(lambda: rows_right().wait_send())
    leave_out(y1, land1, o1_sems)

    own2.wait()
    arrive_out(y2, land2, o2_sems)
    assemble(land2, second_ref)
    leave_out(y2, land2, o2_sems)


def shards(groups, slabs, panels, mean_field, fluctuations, products, triples, owner_slot):
    fields, nnz = 1 + fluctuations.shape[0], products.shape[0]
    entries = -(-nnz // 128) * 128
    panel_planes = jnp.transpose(panels, (1, 0, 2))
    vmem = pl.BlockSpec(memory_space=pltpu.VMEM)
    out = jax.ShapeDtypeStruct(panel_planes.shape, jnp.bfloat16)
    bf16, f32 = jnp.bfloat16, jnp.float32
    dma = pltpu.SemaphoreType.DMA
    first, second = pl.pallas_call(
        functools.partial(kernel, groups, slabs, fields, nnz),
        out_shape=(out, out),
        in_specs=[vmem] * 6,
        out_specs=(vmem, vmem),
        scratch_shapes=[
            pltpu.VMEM((groups, 3, PAD, WIN), bf16),
            pltpu.VMEM((5, ROWS, WIN), bf16),
            pltpu.VMEM((5, ROWS, WIN), bf16),
            pltpu.VMEM((ROWS, FLAT), bf16),
            pltpu.VMEM((ROWS, FLAT), bf16),
            pltpu.VMEM((ROWS, 256), bf16),
            pltpu.VMEM((ROWS, 256), bf16),
            pltpu.VMEM((ROWS, 256), bf16),
            pltpu.VMEM((ROWS, 256), bf16),
            pltpu.VMEM((groups, PAD, FLAT), bf16),
            pltpu.VMEM((groups, PAD, FLAT), bf16),
            pltpu.VMEM((3, 8, WIN), f32),
            pltpu.VMEM((8, WIN), f32),
            pltpu.VMEM((8, WIN), f32),
            pltpu.VMEM((fields, 6, 16, FLAT), CALC),
            pltpu.VMEM((6, 16, FLAT), CALC),
            pltpu.VMEM((3 * ROWS, entries), bf16),
            pltpu.VMEM((ROWS, entries), bf16),
            pltpu.VMEM((ROWS, fields * ROWS), bf16),
            pltpu.VMEM((fields * ROWS, FLAT), bf16),
            dma((groups,)), dma((groups,)), dma,
            dma((2 * groups,)), dma((2 * groups,)), dma((2,)), dma((2,)), dma((2,)), dma((2,)),
            dma((groups,)), dma((groups,)), dma((groups,)), dma((groups,)),
            dma((2 * groups,)), dma((2 * groups,)),
        ],
        compiler_params=pltpu.CompilerParams(
            collective_id=0, has_side_effects=True, vmem_limit_bytes=48 * 1024 * 1024
        ),
    )(panel_planes, mean_field, fluctuations, triples.T, products[None, :], owner_slot[:, None])
    return jnp.transpose(first, (1, 0, 2)), jnp.transpose(second, (1, 0, 2))


def solution(mesh):
    in_specs = (P("chaos", "space", None), P("space", None), P(None, "space", None), P(), P(), P())
    out_specs = (P("chaos", "space", None), P("chaos", "space", None))
    body = functools.partial(shards, mesh.shape["chaos"], mesh.shape["space"])
    return jax.shard_map(body, mesh=mesh, in_specs=in_specs, out_specs=out_specs, check_vma=False)
```

time: 221 us -> 45.2 us (0.20)
  waiting for transfers between devices: 81.6 us -> 0 us
  local copies, waits for them, and re-layouts: 54.2 us -> 4.94 us
  other arithmetic: 43 us -> 0 us
  Pallas kernels: 0 us -> 38.9 us
  starting transfers between devices: 20.5 us -> 0 us
  between operations: 14.5 us -> 0.67 us
  matrix products: 6.38 us -> 0 us
    ppermute x6 -> x0, waiting for transfers between devices: 48.5 us -> none  [the longest x3 36.4 us: padded(): lax.ppermute(lax.slice_in_dim(block, 0, width, axis=dim), axis, backward)]
    pallas_call x0 -> x1, Pallas kernels: none -> 38.9 us  [shards(): pl.pallas_call(functools.partial(kernel, groups, slabs, fields, nnz), out...]
    all_gather x2 -> x0, waiting for transfers between devices: 33.1 us -> none  [combine(): lax.all_gather(own_panels, 'chaos', axis=0, tiled=True)]
    slice x42 -> x0, local copies, waits for them, and re-layouts: 30.8 us -> none  [the longest x36 28.5 us: shifted(): moved_values = jnp.pad(source[..., offset:], padding + [(0, offset)])]
    convert_element_type x5 -> x0, other arithmetic: 27.2 us -> none  [the longest x2 24.6 us: galerkin_apply(): return (scale_factor * result).astype(jnp.bfloat16)]
    ppermute x6 -> x0, starting transfers between devices: 20.4 us -> none  [the longest x3 14.2 us: padded(): lax.ppermute(lax.slice_in_dim(block, 0, width, axis=dim), axis, backward)]
    gather x2 -> x0, local copies, waits for them, and re-layouts: 16 us -> none  [the longest x1 7.98 us: shards(): column_slot = owner_slot[triples[:, 1]]]
    unnamed x4 -> x0, other arithmetic: 7.96 us -> none
  transfers between devices with their start and end apart: 8 -> 0, of which waited for: 6 -> 0; matrix products, arithmetic and copies ran while one was open for 16% -> 0% of each run, Pallas kernels for 0% -> 0%
where the time goes in v2:
time: 45.2 us; the launch traced here: 44.5 us
  Pallas kernels  38.9 us (86%)
  local copies, waits for them, and re-layouts  4.94 us (11%)
  between operations  0.67 us (1%)
    pallas_call x1, Pallas kernels, shards(): pl.pallas_call(functools.partial(kernel, groups, slabs, fields, nnz), out...  38.9 us
    unnamed x12, local copies, waits for them, and re-layouts  4.11 us

profile of v2, /device:TPU:7, one launch (start us, length us, event | category | flops | bytes accessed | tf_op | source)
XLA Modules:
  0.0 44.5 jit_solution(8346551087806807359)
XLA Ops:
  0.6 0.0 copy-start.4
  0.6 0.7 %broadcast_in_dim.6.product_ref = f32[1,1218]{1,0:T(1,128)S(1)} reshape(f32[1218]{0:T(1024)} %param.9) | data formatting | bytes 9744 | tf_op jit(solution)/shard_map/broadcast_in_dim | solution.py:469
  1.3 0.0 copy-done.4
  1.4 0.0 copy-start.2
  1.4 0.0 copy-start.3
  1.4 0.1 copy.8.slot_ref
  1.5 0.6 %copy-done.2 = f32[3,2304]{1,0:T(4,128)S(1)} copy-done((f32[3,2304]{1,0:T(4,128)S(1)}, f32[3,2304]{1,0:T(4,128)}, u32[]{:S(2)}) %copy-start.2) | copy-done | bytes 27672
  2.1 0.0 copy-done.3
  2.1 0.0 copy-start
  2.1 1.0 %copy-done = bf16[27,3,2304]{2,0,1:T(8,128)(2,1)S(1)} copy-done((bf16[27,3,2304]{2,0,1:T(8,128)(2,1)S(1)}, bf16[27,3,2304]{2,0,1:T(8,128)(2,1)}, u32[]{:S(2)}) %copy-start) | copy-done | bytes 373272
  3.1 0.0 copy-start.1
  3.1 0.9 %copy-done.1 = f32[6,3,2304]{2,1,0:T(4,128)S(1)} copy-done((f32[6,3,2304]{2,1,0:T(4,128)S(1)}, f32[6,3,2304]{2,1,0:T(4,128)}, u32[]{:S(2)}) %copy-start.1) | copy-done | bytes 165912
  4.1 38.9 %shard_map.77 = (bf16[3,27,2304]{2,1,0:T(8,128)(2,1)S(1)}, bf16[3,27,2304]{2,1,0:T(8,128)(2,1)S(1)}) custom-call(bf16[3,27,2304]{2,1,0:T(8,128)(2,1)S(1)} %bitcast.5, f32[3,2304]{1,0:T(4,128)S(1)} %copy-done.2, f32[6,3,2304]{2,1,0:T(4,128)S(1)} %copy-done.1, s32[3,1218]{1,0:T(4,128)S(1)} %bitcast.8, f32[1,1218]{1,0:T(1,128)S(1)} %broadcast_in_dim.6.product_ref, ...), custom_call_target="tpu_custom_call" | custom-call | tf_op jit(solution)/shard_map/pallas_call | solution.py:435
  43.0 0.8 %copy.11 = bf16[27,3,2304]{2,0,1:T(8,128)(2,1)} copy(bf16[27,3,2304]{2,0,1:T(8,128)(2,1)S(1)} %bitcast.7) | data formatting | bytes 746496
  43.8 0.8 %copy.12 = bf16[27,3,2304]{2,0,1:T(8,128)(2,1)} copy(bf16[27,3,2304]{2,0,1:T(8,128)(2,1)S(1)} %bitcast.6) | data formatting | bytes 746496
Async XLA Ops:
  0.6 0.7 %copy-start.4 = (s32[210]{0:T(256)S(1)}, s32[210]{0:T(256)}, u32[]{:S(2)}) copy-start(s32[210]{0:T(256)} %param.11) | copy-start | bytes 2524
  1.4 0.8 %copy-start.2 = (f32[3,2304]{1,0:T(4,128)S(1)}, f32[3,2304]{1,0:T(4,128)}, u32[]{:S(2)}) copy-start(f32[3,2304]{1,0:T(4,128)} %mean_ref.1) | copy-start | bytes 82948
  1.4 0.8 %copy-start.3 = (s32[1218,3]{0,1:T(4,128)S(1)}, s32[1218,3]{0,1:T(4,128)}, u32[]{:S(2)}) copy-start(s32[1218,3]{0,1:T(4,128)} %param.10) | copy-start | bytes 43852
  2.1 1.0 %copy-start = (bf16[27,3,2304]{2,0,1:T(8,128)(2,1)S(1)}, bf16[27,3,2304]{2,0,1:T(8,128)(2,1)}, u32[]{:S(2)}) copy-start(bf16[27,3,2304]{2,0,1:T(8,128)(2,1)} %param.6) | copy-start | bytes 1119748
  3.1 0.9 %copy-start.1 = (f32[6,3,2304]{2,1,0:T(4,128)S(1)}, f32[6,3,2304]{2,1,0:T(4,128)}, u32[]{:S(2)}) copy-start(f32[6,3,2304]{2,1,0:T(4,128)} %fluct_ref.1) | copy-start | bytes 497668

commit v3 on v2

--- a/solution.py
+++ b/solution.py
@@ -15,7 +15,9 @@
 PAD = 32
 ROWS = 256
 HALF = 0.5 * 0.15
-CALC = jnp.bfloat16
+
+AT = (0, 2, 1)
+SEND = (1, 2, 3, 4, 6, 5, 7)
 
 ORDER = ((0, 0), (0, 1), (2, 0), (2, 1), (1, 0), (1, 1), (3, 0), (3, 1))
 
@@ -52,11 +54,12 @@
 
 def kernel(
     groups, slabs, fields, nnz,
-    panel_ref, mean_ref, fluct_ref, triple_ref, product_ref, slot_ref,
+    panel_hbm, mean_hbm, fluct_hbm, triple_hbm, product_hbm, slot_hbm,
     first_ref, second_ref,
+    panel_ref, mean_ref, fluct_ref, triple_ref, product_ref, slot_ref, load_sem,
     send_buf, x1, x2, y1, y2, edge_low, edge_high, halo_low, halo_high, land1, land2,
-    coef, coef_low, coef_high, weight, drops, onehot_rows, onehot_cols, table, scaled,
-    a2a_send, a2a_recv, self_sem, z_send, z_recv, c_send, c_recv,
+    coef, coef_low, coef_high, weight, keep, lines, drops, onehot_rows, onehot_cols, table, scaled,
+    a2a_send, a2a_recv, mid_send, mid_recv, self_sem, mid_sem, z_send, z_recv, c_send, c_recv,
     h_send, h_recv, o1_send, o1_recv, o2_send, o2_recv, z2_send, z2_recv,
 ):
     part = lax.axis_index("chaos")
@@ -71,6 +74,18 @@
         far, other = ORDER[step]
         return lax.rem(chip + far, groups // 2) * 2 + lax.rem(core + other, 2)
 
+    loads = [
+        pltpu.make_async_copy(source, target, load_sem.at[index])
+        for index, (source, target) in enumerate(
+            (
+                (panel_hbm, panel_ref), (mean_hbm, mean_ref), (fluct_hbm, fluct_ref),
+                (triple_hbm, triple_ref), (product_hbm, product_ref), (slot_hbm, slot_ref),
+            )
+        )
+    ]
+    for load in loads:
+        load.start()
+
     barrier = pltpu.get_barrier_semaphore()
     for step in range(1, groups):
         pl.semaphore_signal(barrier, inc=1, device_id=(group_of(step), slab), device_id_type=MESH)
@@ -86,12 +101,19 @@
     lane = lax.broadcasted_iota(jnp.int32, (1, WIN), 1)
     tile_lane = lax.broadcasted_iota(jnp.int32, (1, 128), 1)
     send_buf[:, :, 16:32, :] = jnp.zeros((groups, 3, 16, WIN), bf16)
+    for plane in range(3):
+        cell = lax.rem(lax.broadcasted_iota(jnp.int32, (16, WIN), 1) + (WIN - 32 * plane), SIDE)
+        keep[plane, 0] = jnp.where(cell < SIDE - 1, 1.0, 0.0).astype(bf16)
+        keep[plane, 1] = jnp.where(cell > 0, 1.0, 0.0).astype(bf16)
+    loads[0].wait()
     for target in range(groups):
         for plane in range(3):
             block = linear_window(panel_ref, (plane, slice(None)), target, lane)
             block = pltpu.roll(block, (32 * plane - SIDE) % WIN, 1)
-            send_buf[target, plane, 0:own_rows, :] = block.astype(bf16)
-
+            send_buf[target, AT[plane], 0:own_rows, :] = block.astype(bf16)
+
+    for load in loads[1:]:
+        load.wait()
     coef[...] = jnp.zeros_like(coef)
     for target in range(groups):
         @pl.when(part == target)
@@ -110,18 +132,34 @@
 
     def a2a(peer, source):
         return pltpu.make_async_remote_copy(
-            src_ref=send_buf.at[peer],
-            dst_ref=x1.at[pl.ds(1, 3), rows_of(source), :],
+            src_ref=send_buf.at[peer, pl.ds(0, 2)],
+            dst_ref=x1.at[pl.ds(1, 2), rows_of(source), :],
             send_sem=a2a_send.at[peer],
             recv_sem=a2a_recv.at[source],
             device_id=(peer, slab),
             device_id_type=MESH,
         )
 
-    own = pltpu.make_async_copy(send_buf.at[part], x1.at[pl.ds(1, 3), rows_of(part), :], self_sem)
+    def a2a_middle(peer, source):
+        return pltpu.make_async_remote_copy(
+            src_ref=send_buf.at[peer, 2],
+            dst_ref=x1.at[3, rows_of(source), :],
+            send_sem=mid_send.at[peer],
+            recv_sem=mid_recv.at[source],
+            device_id=(peer, slab),
+            device_id_type=MESH,
+        )
+
+    own = pltpu.make_async_copy(
+        send_buf.at[part, pl.ds(0, 2)], x1.at[pl.ds(1, 2), rows_of(part), :], self_sem
+    )
+    own_middle = pltpu.make_async_copy(send_buf.at[part, 2], x1.at[3, rows_of(part), :], mid_sem)
     own.start()
-    for step in (2, 3, 4, 5, 6, 7, 1):
+    own_middle.start()
+    for step in SEND:
         a2a(group_of(step), part).start()
+    for step in SEND:
+        a2a_middle(group_of(step), part).start()
 
     def to_slab(source, target, sems, index, other):
         return pltpu.make_async_remote_copy(
@@ -129,9 +167,15 @@
             device_id=(part, other), device_id_type=MESH,
         )
 
+    def start_low(low):
+        pl.when(has_low)(lambda: low().start())
+
+    def start_high(high):
+        pl.when(has_high)(lambda: high().start())
+
     def start_planes(low, high):
-        pl.when(has_low)(lambda: low().start())
-        pl.when(has_high)(lambda: high().start())
+        start_low(low)
+        start_high(high)
 
     def arrive_planes(low, high):
         pl.when(has_low)(lambda: high().wait_recv())
@@ -172,7 +216,7 @@
         rows = rows_of(group)
         return (
             lambda: to_slab(x1.at[1, rows, :], x1.at[4, rows, :], z_sems, group, slab - 1),
-            lambda: to_slab(x1.at[3, rows, :], x1.at[0, rows, :], z_sems, groups + group, slab + 1),
+            lambda: to_slab(x1.at[2, rows, :], x1.at[0, rows, :], z_sems, groups + group, slab + 1),
         )
 
     def y_planes(group):
@@ -184,48 +228,74 @@
             ),
         )
 
-    own.wait()
-    start_planes(*x_planes(part))
-
-    slot = slot_ref[...]
+    def pass_on(step):
+        group = group_of(step)
+        if step:
+            a2a(part, group).wait_recv()
+        else:
+            own.wait()
+        start_planes(*x_planes(group))
+
+    pass_on(0)
+
+    slot = slot_ref[...].reshape(1, slot_ref.shape[0])
     slot = slot + (PAD - own_rows) * (slot // own_rows)
-    name = lax.broadcasted_iota(jnp.int32, slot.shape, 0)
+    slot = jnp.broadcast_to(slot.astype(f32), (8, slot_ref.shape[0])).astype(bf16)
+    name = lax.broadcasted_iota(jnp.int32, (slot_ref.shape[0], nnz), 0)
 
     def slots(index):
-        hit = name == triple_ref[index : index + 1, :]
-        return jnp.sum(jnp.where(hit, slot, 0), axis=0, keepdims=True)
-
-    row = slots(0)
-    column = slots(1) + ROWS * triple_ref[2:3, :]
-    value = product_ref[...]
+        hit = jnp.where(name == triple_ref[index : index + 1, :], 1.0, 0.0).astype(bf16)
+        return jnp.dot(slot, hit, preferred_element_type=f32)[0:1]
+
+    def wide(line):
+        return jnp.broadcast_to(line, (16, nnz)).astype(bf16)
+
+    lines[0, :, 0:nnz] = wide(slots(0))
+    column = slots(1)
+    value = product_ref[...].reshape(1, nnz)
     top = value.astype(bf16).astype(f32)
-    middle = (value - top).astype(bf16).astype(f32)
-    bottom = value - top - middle
+    lines[1, :, 0:nnz] = wide(top)
+    lines[2, :, 0:nnz] = wide(value - top)
+    for field in range(fields):
+        lines[3 + field, :, 0:nnz] = wide(jnp.where(triple_ref[2:3, :] == field, column, -1.0))
     last_tile = slice(nnz // 128 * 128, nnz // 128 * 128 + 128)
-    onehot_rows[:, last_tile] = jnp.zeros((3 * ROWS, 128), bf16)
+    onehot_rows[:, last_tile] = jnp.zeros((2 * ROWS, 128), bf16)
     onehot_cols[:, last_tile] = jnp.zeros((ROWS, 128), bf16)
+    numbers = lax.broadcasted_iota(jnp.int32, (16, nnz), 0).astype(f32).astype(bf16)
+
+    def spread(line, block, values, target, base):
+        at = pl.ds(pl.multiple_of(base + block * 16, 16), 16)
+        start = (block * 16).astype(f32).astype(bf16)
+        target[at, 0:nnz] = jnp.where(line - start == numbers, values, jnp.zeros_like(values))
 
     @pl.loop(0, 16)
     def _(block):
-        hit = row == lax.broadcasted_iota(jnp.int32, (16, nnz), 0) + block * 16
-        for piece, part_value in enumerate((top, middle, bottom)):
-            at = pl.ds(pl.multiple_of(piece * ROWS + block * 16, 16), 16)
-            onehot_rows[at, 0:nnz] = jnp.where(hit, part_value, 0.0).astype(bf16)
-
-    @pl.loop(0, fields)
-    def _(field):
-        @pl.loop(0, 16)
-        def _(block):
-            index = lax.broadcasted_iota(jnp.int32, (16, nnz), 0) + (field * ROWS + block * 16)
-            at = pl.ds(pl.multiple_of(block * 16, 16), 16)
-            onehot_cols[at, 0:nnz] = jnp.where(column == index, 1.0, 0.0).astype(bf16)
-
-        pieces = lax.dot_general(
-            onehot_rows[...], onehot_cols[...], (((1,), (1,)), ((), ())), preferred_element_type=f32
-        )
-        table[:, pl.ds(pl.multiple_of(field * ROWS, ROWS), ROWS)] = (
-            pieces[0:256] + pieces[256:512] + pieces[512:768]
-        ).astype(bf16)
+        spread(lines[0, :, 0:nnz], block, lines[1, :, 0:nnz], onehot_rows, 0)
+        spread(lines[0, :, 0:nnz], block, lines[2, :, 0:nnz], onehot_rows, ROWS)
+
+    def tabulate(start, stop):
+        @pl.loop(start, stop)
+        def _(field):
+            @pl.loop(0, 16)
+            def _(block):
+                ones = jnp.ones((16, nnz), bf16)
+                spread(lines[3 + field, :, 0:nnz], block, ones, onehot_cols, 0)
+
+            pieces = lax.dot_general(
+                onehot_rows[...], onehot_cols[...], (((1,), (1,)), ((), ())), preferred_element_type=f32
+            )
+            table[:, pl.ds(pl.multiple_of(field * ROWS, ROWS), ROWS)] = (
+                pieces[0:ROWS] + pieces[ROWS:]
+            ).astype(bf16)
+
+    tabulate(0, 2)
+    pass_on(1)
+    tabulate(2, 4)
+    pass_on(2)
+    pass_on(3)
+    tabulate(4, 6)
+    pass_on(4)
+    pass_on(6)
 
     arrive_planes(*coef_copies)
     inside = []
@@ -254,56 +324,75 @@
     for face in range(6):
         half = flatten([halves[plane][face] for plane in range(3)], tile_lane)
         for field in range(fields):
-            weight[field, face] = jnp.broadcast_to(half[field : field + 1], (16, FLAT)).astype(CALC)
-
-    def scale(x, start):
-        at = pl.ds(pl.multiple_of(start, 16), 16)
-        own_planes = [x[plane + 1, at, :].astype(f32) for plane in range(3)]
-        faces = []
-        for plane in range(3):
-            here = own_planes[plane]
-            if plane == 2:
-                above = pltpu.roll(x[4, at, :].astype(f32), 64, 1)
-            else:
-                above = pltpu.roll(own_planes[plane + 1], WIN - 32, 1)
-            if plane == 0:
-                below = pltpu.roll(x[0, at, :].astype(f32), WIN - 64, 1)
-            else:
-                below = pltpu.roll(own_planes[plane - 1], 32, 1)
-            faces.append([here - side for side in neighbours(here, plane, above, below)])
-        for face in range(6):
-            drops[face] = flatten([faces[plane][face] for plane in range(3)], tile_lane).astype(CALC)
-        for first in range(0, FLAT, 256):
-            lanes = slice(first, min(first + 256, FLAT))
-            drop = [drops[face, :, lanes] for face in range(6)]
-            for field in range(fields):
-                terms = [weight[field, face, :, lanes] * drop[face] for face in range(6)]
-                flux = (terms[0] + terms[1]) + (terms[2] + terms[3]) + (terms[4] + terms[5])
-                to = pl.ds(pl.multiple_of(field * ROWS + start, 16), 16)
-                scaled[to, lanes] = flux.astype(bf16)
+            weight[field, face] = jnp.broadcast_to(half[field : field + 1], (8, FLAT)).astype(bf16)
+
+    pass_on(5)
+    pass_on(7)
+    tabulate(6, 7)
 
     def scale_group(x, group):
-        @pl.loop(0, PAD // 16)
-        def _(block):
-            scale(x, group * PAD + block * 16)
-
-    def combine(y):
-        for first in range(0, FLAT, 256):
-            lanes = slice(first, min(first + 256, FLAT))
+        for block in range(PAD // 16):
+            at = pl.ds(pl.multiple_of(group * PAD + block * 16, 16), 16)
+            to = slice(block * 16, block * 16 + 16)
+            own_planes = [x[1 + AT[plane], at, :] for plane in range(3)]
+            for plane in range(3):
+                here = own_planes[plane]
+                if plane == 2:
+                    above = pltpu.roll(x[4, at, :], 64, 1)
+                else:
+                    above = pltpu.roll(own_planes[plane + 1], WIN - 32, 1)
+                if plane == 0:
+                    below = pltpu.roll(x[0, at, :], WIN - 64, 1)
+                else:
+                    below = pltpu.roll(own_planes[plane - 1], 32, 1)
+                sides = (
+                    pltpu.roll(here, WIN - 1, 1) * keep[plane, 0],
+                    pltpu.roll(here, 1, 1) * keep[plane, 1],
+                    pltpu.roll(here, WIN - SIDE, 1),
+                    pltpu.roll(here, SIDE, 1),
+                    above,
+                    below,
+                )
+                for face, side in enumerate(sides):
+                    drop = here - side
+                    first, cut = CELLS * plane - 32 * plane, 32 * plane
+                    for low in (0, 128, 256):
+                        begin, end = max(low, cut), min(low + 128, cut + CELLS)
+                        if plane == 2 and low == 256:
+                            end = WIN
+                        drops[face, to, first + begin : first + end] = drop[:, begin:end]
+
+        @pl.when(group >= 0)
+        def _():
+            for first in range(0, FLAT, 256):
+                lanes = slice(first, min(first + 256, FLAT))
+                drop = [drops[face, :, lanes].reshape(PAD // 8, 8, -1) for face in range(6)]
+                for field in range(fields):
+                    terms = [weight[field, face, :, lanes] * drop[face] for face in range(6)]
+                    flux = (terms[0] + terms[1]) + (terms[2] + terms[3]) + (terms[4] + terms[5])
+                    to = pl.ds(pl.multiple_of(field * ROWS + group * PAD, PAD), PAD)
+                    scaled[to, lanes] = flux.reshape(PAD, -1)
+
+    def combine(y, first):
+        for start in (first, first + 256):
+            lanes = slice(start, min(start + 256, FLAT))
             y[:, lanes] = jnp.dot(table[...], scaled[:, lanes], preferred_element_type=f32).astype(bf16)
 
-    for step in range(1, groups):
-        group = group_of(step)
-        a2a(part, group).wait_recv()
-        start_planes(*x_planes(group))
-    for step in range(groups):
+    for step in (0, 1, 2, 3, 4, 6, 5, 7):
         group = group_of(step)
         arrive_planes(*x_planes(group))
+        if step:
+            a2a_middle(part, group).wait_recv()
+        else:
+            own_middle.wait()
         scale_group(x1, group)
-    combine(y1)
-
+    combine(y1, 0)
     for step in range(groups):
-        start_planes(*y_planes(group_of(step)))
+        start_low(y_planes(group_of(step))[0])
+    combine(y1, 512)
+
+    for step in range(groups):
+        start_high(y_planes(group_of(step))[1])
 
     @pl.loop(0, 16)
     def _(block):
@@ -329,32 +418,33 @@
     pl.when(left)(lambda: rows_left().start())
     pl.when(right)(lambda: rows_right().start())
 
-    def out_copy(y, land, peer, source, sems):
+    def out_copy(y, land, peer, source, sems, lanes=(0, FLAT), shift=0):
+        window = pl.ds(lanes[0], lanes[1])
         return pltpu.make_async_remote_copy(
-            src_ref=y.at[rows_of(peer), :], dst_ref=land.at[source],
-            send_sem=sems[0].at[peer], recv_sem=sems[1].at[source],
+            src_ref=y.at[rows_of(peer), window], dst_ref=land.at[source, :, window],
+            send_sem=sems[0].at[shift + peer], recv_sem=sems[1].at[shift + source],
             device_id=(peer, slab), device_id_type=MESH,
         )
 
-    def start_out(y, land, sems):
-        for step in (2, 3, 4, 5, 6, 7, 1):
-            out_copy(y, land, group_of(step), part, sems).start()
-
-    def leave_out(y, land, sems):
+    def start_out(y, land, sems, *how):
+        for step in (2, 3, 4, 6, 5, 7, 1):
+            out_copy(y, land, group_of(step), part, sems, *how).start()
+
+    def leave_out(y, land, sems, *how):
         for step in range(1, groups):
-            out_copy(y, land, group_of(step), part, sems).wait_send()
-
-    def arrive_out(y, land, sems):
+            out_copy(y, land, group_of(step), part, sems, *how).wait_send()
+
+    def arrive_out(y, land, sems, *how):
         for step in range(1, groups):
-            out_copy(y, land, part, group_of(step), sems).wait_recv()
+            out_copy(y, land, part, group_of(step), sems, *how).wait_recv()
 
     o1_sems, o2_sems = (o1_send, o1_recv), (o2_send, o2_recv)
+    pl.when(left)(lambda: rows_right().wait_recv())
+    pl.when(right)(lambda: rows_left().wait_recv())
+
     start_out(y1, land1, o1_sems)
     own1 = pltpu.make_async_copy(y1.at[rows_of(part), :], land1.at[part], self_sem)
     own1.start()
-
-    pl.when(left)(lambda: rows_right().wait_recv())
-    pl.when(right)(lambda: rows_left().wait_recv())
 
     @pl.loop(0, 16)
     def _(block):
@@ -366,23 +456,26 @@
         x2[1, at, 256:384] = jnp.where(
             tile_lane < 32, tile[0], jnp.where(tile_lane < 80, high, low)
         ).astype(bf16)
-        x2[2, at, 0:128] = jnp.where(tile_lane < 32, low_b, tile[0]).astype(bf16)
-        x2[2, at, 128:256] = y1[at, 384:512]
-        x2[2, at, 256:384] = jnp.where(
+        x2[3, at, 0:128] = jnp.where(tile_lane < 32, low_b, tile[0]).astype(bf16)
+        x2[3, at, 128:256] = y1[at, 384:512]
+        x2[3, at, 256:384] = jnp.where(
             tile_lane < 64, tile[1], jnp.where(tile_lane < 112, high_b, low_b)
         ).astype(bf16)
-        x2[3, at, 0:128] = jnp.where(
+        x2[2, at, 0:128] = jnp.where(
             tile_lane < 16, high, jnp.where(tile_lane < 64, low, tile[1])
         ).astype(bf16)
-        x2[3, at, 128:256] = y1[at, 640:768]
-        x2[3, at, 256:384] = jnp.where(tile_lane < 96, tile[2], high).astype(bf16)
+        x2[2, at, 128:256] = y1[at, 640:768]
+        x2[2, at, 256:384] = jnp.where(tile_lane < 96, tile[2], high).astype(bf16)
 
     for step in range(groups):
         group = group_of(step)
         arrive_planes(*y_planes(group))
         scale_group(x2, group)
-    combine(y2)
-    start_out(y2, land2, o2_sems)
+    begin, end = ((0, 512), 0), ((512, FLAT - 512), groups)
+    combine(y2, 0)
+    start_out(y2, land2, o2_sems, *begin)
+    combine(y2, 512)
+    start_out(y2, land2, o2_sems, *end)
     own1.wait()
     own2 = pltpu.make_async_copy(y2.at[rows_of(part), :], land2.at[part], self_sem)
     own2.start()
@@ -414,14 +507,17 @@
         leave_planes(*y_planes(group_of(step)))
     for step in range(1, groups):
         a2a(group_of(step), part).wait_send()
+        a2a_middle(group_of(step), part).wait_send()
     pl.when(left)(lambda: rows_left().wait_send())
     pl.when(right)(lambda: rows_right().wait_send())
     leave_out(y1, land1, o1_sems)
 
     own2.wait()
-    arrive_out(y2, land2, o2_sems)
+    for how in (begin, end):
+        arrive_out(y2, land2, o2_sems, *how)
     assemble(land2, second_ref)
-    leave_out(y2, land2, o2_sems)
+    for how in (begin, end):
+        leave_out(y2, land2, o2_sems, *how)
 
 
 def shards(groups, slabs, panels, mean_field, fluctuations, products, triples, owner_slot):
@@ -432,12 +528,20 @@
     out = jax.ShapeDtypeStruct(panel_planes.shape, jnp.bfloat16)
     bf16, f32 = jnp.bfloat16, jnp.float32
     dma = pltpu.SemaphoreType.DMA
+    operands = (panel_planes, mean_field, fluctuations, triples.T, products, owner_slot)
     first, second = pl.pallas_call(
         functools.partial(kernel, groups, slabs, fields, nnz),
         out_shape=(out, out),
-        in_specs=[vmem] * 6,
+        in_specs=[pl.BlockSpec(memory_space=pltpu.HBM)] * 6,
         out_specs=(vmem, vmem),
         scratch_shapes=[
+            pltpu.VMEM(panel_planes.shape, bf16),
+            pltpu.VMEM(mean_field.shape, f32),
+            pltpu.VMEM(fluctuations.shape, f32),
+            pltpu.VMEM((3, nnz), jnp.int32),
+            pltpu.VMEM((nnz,), f32),
+            pltpu.VMEM(owner_slot.shape, jnp.int32),
+            dma((6,)),
             pltpu.VMEM((groups, 3, PAD, WIN), bf16),
             pltpu.VMEM((5, ROWS, WIN), bf16),
             pltpu.VMEM((5, ROWS, WIN), bf16),
@@ -452,21 +556,23 @@
             pltpu.VMEM((3, 8, WIN), f32),
             pltpu.VMEM((8, WIN), f32),
             pltpu.VMEM((8, WIN), f32),
-            pltpu.VMEM((fields, 6, 16, FLAT), CALC),
-            pltpu.VMEM((6, 16, FLAT), CALC),
-            pltpu.VMEM((3 * ROWS, entries), bf16),
+            pltpu.VMEM((fields, 6, 8, FLAT), bf16),
+            pltpu.VMEM((3, 2, 16, WIN), bf16),
+            pltpu.VMEM((3 + fields, 16, entries), bf16),
+            pltpu.VMEM((6, PAD, FLAT), bf16),
+            pltpu.VMEM((2 * ROWS, entries), bf16),
             pltpu.VMEM((ROWS, entries), bf16),
             pltpu.VMEM((ROWS, fields * ROWS), bf16),
             pltpu.VMEM((fields * ROWS, FLAT), bf16),
-            dma((groups,)), dma((groups,)), dma,
+            dma((groups,)), dma((groups,)), dma((groups,)), dma((groups,)), dma, dma,
             dma((2 * groups,)), dma((2 * groups,)), dma((2,)), dma((2,)), dma((2,)), dma((2,)),
-            dma((groups,)), dma((groups,)), dma((groups,)), dma((groups,)),
+            dma((groups,)), dma((groups,)), dma((2 * groups,)), dma((2 * groups,)),
             dma((2 * groups,)), dma((2 * groups,)),
         ],
         compiler_params=pltpu.CompilerParams(
             collective_id=0, has_side_effects=True, vmem_limit_bytes=48 * 1024 * 1024
         ),
-    )(panel_planes, mean_field, fluctuations, triples.T, products[None, :], owner_slot[:, None])
+    )(*(pltpu.with_memory_space_constraint(operand, pltpu.HBM) for operand in operands))
     return jnp.transpose(first, (1, 0, 2)), jnp.transpose(second, (1, 0, 2))
 
 

time: 45.2 us -> 41.5 us (0.918); the launches traced: 44.5 us -> 41.3 us
  local copies, waits for them, and re-layouts: 4.94 us -> 1.53 us
    unnamed x12 -> x2, local copies, waits for them, and re-layouts: 4.11 us -> 1.53 us
    broadcast_in_dim x2 -> x0, local copies, waits for them, and re-layouts: 0.83 us -> none  [the longest x1 0.71 us: shards(): products[None, :]]
where the time goes in v3:
time: 41.5 us; the launch traced here: 41.3 us
  Pallas kernels  39.2 us (94%)
  local copies, waits for them, and re-layouts  1.53 us (4%)
  between operations  0.64 us (2%)
    pallas_call x1, Pallas kernels, shards(): pl.pallas_call(functools.partial(kernel, groups, slabs, fields, nnz), out...  39.2 us
    unnamed x2, local copies, waits for them, and re-layouts  1.53 us

profile of v3, /device:TPU:7, one launch (start us, length us, event | category | flops | bytes accessed | tf_op | source)
XLA Modules:
  0.0 41.3 jit_solution(18321795472744476644)
XLA Ops:
  0.6 39.2 %shard_map.77 = (bf16[3,27,2304]{2,1,0:T(8,128)(2,1)S(1)}, bf16[3,27,2304]{2,1,0:T(8,128)(2,1)S(1)}) custom-call(bf16[3,27,2304]{2,1,0:T(8,128)(2,1)} %bitcast.6, f32[3,2304]{1,0:T(4,128)} %mean_hbm.1, f32[6,3,2304]{2,1,0:T(4,128)} %fluct_hbm.1, s32[3,1218]{1,0:T(4,128)} %bitcast.7, f32[1218]{0:T(1024)} %product_hbm.1, s32[210]{0:T(256)} %slot_hbm.1), custom_call_target="tpu_custom_call" | custom-call | tf_op jit(solution)/shard_map/pallas_call | solution.py:532
  39.8 0.8 %copy.10 = bf16[27,3,2304]{2,0,1:T(8,128)(2,1)} copy(bf16[27,3,2304]{2,0,1:T(8,128)(2,1)S(1)} %bitcast.5) | data formatting | bytes 746496
  40.6 0.8 %copy.11 = bf16[27,3,2304]{2,0,1:T(8,128)(2,1)} copy(bf16[27,3,2304]{2,0,1:T(8,128)(2,1)S(1)} %bitcast.4) | data formatting | bytes 746496

commit v4 on v3

--- a/solution.py
+++ b/solution.py
@@ -18,6 +18,7 @@
 
 AT = (0, 2, 1)
 SEND = (1, 2, 3, 4, 6, 5, 7)
+OUT1 = 2
 
 ORDER = ((0, 0), (0, 1), (2, 0), (2, 1), (1, 0), (1, 1), (3, 0), (3, 1))
 
@@ -112,6 +113,42 @@
             block = pltpu.roll(block, (32 * plane - SIDE) % WIN, 1)
             send_buf[target, AT[plane], 0:own_rows, :] = block.astype(bf16)
 
+    pl.semaphore_wait(barrier, groups - 1 + has_low.astype(jnp.int32) + has_high.astype(jnp.int32))
+
+    def rows_of(group):
+        return pl.ds(pl.multiple_of(group * PAD, PAD), PAD)
+
+    def a2a(peer, source):
+        return pltpu.make_async_remote_copy(
+            src_ref=send_buf.at[peer, pl.ds(0, 2)],
+            dst_ref=x1.at[pl.ds(1, 2), rows_of(source), :],
+            send_sem=a2a_send.at[peer],
+            recv_sem=a2a_recv.at[source],
+            device_id=(peer, slab),
+            device_id_type=MESH,
+        )
+
+    def a2a_middle(peer, source):
+        return pltpu.make_async_remote_copy(
+            src_ref=send_buf.at[peer, 2],
+            dst_ref=x1.at[3, rows_of(source), :],
+            send_sem=mid_send.at[peer],
+            recv_sem=mid_recv.at[source],
+            device_id=(peer, slab),
+            device_id_type=MESH,
+        )
+
+    own = pltpu.make_async_copy(
+        send_buf.at[part, pl.ds(0, 2)], x1.at[pl.ds(1, 2), rows_of(part), :], self_sem
+    )
+    own_middle = pltpu.make_async_copy(send_buf.at[part, 2], x1.at[3, rows_of(part), :], mid_sem)
+    own.start()
+    own_middle.start()
+    for step in SEND:
+        a2a(group_of(step), part).start()
+    for step in SEND:
+        a2a_middle(group_of(step), part).start()
+
     for load in loads[1:]:
         load.wait()
     coef[...] = jnp.zeros_like(coef)
@@ -125,42 +162,6 @@
                         fluct_ref, (field - 1, slice(plane, plane + 1)), target, lane
                     )
 
-    pl.semaphore_wait(barrier, groups - 1 + has_low.astype(jnp.int32) + has_high.astype(jnp.int32))
-
-    def rows_of(group):
-        return pl.ds(pl.multiple_of(group * PAD, PAD), PAD)
-
-    def a2a(peer, source):
-        return pltpu.make_async_remote_copy(
-            src_ref=send_buf.at[peer, pl.ds(0, 2)],
-            dst_ref=x1.at[pl.ds(1, 2), rows_of(source), :],
-            send_sem=a2a_send.at[peer],
-            recv_sem=a2a_recv.at[source],
-            device_id=(peer, slab),
-            device_id_type=MESH,
-        )
-
-    def a2a_middle(peer, source):
-        return pltpu.make_async_remote_copy(
-            src_ref=send_buf.at[peer, 2],
-            dst_ref=x1.at[3, rows_of(source), :],
-            send_sem=mid_send.at[peer],
-            recv_sem=mid_recv.at[source],
-            device_id=(peer, slab),
-            device_id_type=MESH,
-        )
-
-    own = pltpu.make_async_copy(
-        send_buf.at[part, pl.ds(0, 2)], x1.at[pl.ds(1, 2), rows_of(part), :], self_sem
-    )
-    own_middle = pltpu.make_async_copy(send_buf.at[part, 2], x1.at[3, rows_of(part), :], mid_sem)
-    own.start()
-    own_middle.start()
-    for step in SEND:
-        a2a(group_of(step), part).start()
-    for step in SEND:
-        a2a_middle(group_of(step), part).start()
-
     def to_slab(source, target, sems, index, other):
         return pltpu.make_async_remote_copy(
             src_ref=source, dst_ref=target, send_sem=sems[0].at[index], recv_sem=sems[1].at[index],
@@ -268,18 +269,20 @@
         start = (block * 16).astype(f32).astype(bf16)
         target[at, 0:nnz] = jnp.where(line - start == numbers, values, jnp.zeros_like(values))
 
-    @pl.loop(0, 16)
-    def _(block):
-        spread(lines[0, :, 0:nnz], block, lines[1, :, 0:nnz], onehot_rows, 0)
-        spread(lines[0, :, 0:nnz], block, lines[2, :, 0:nnz], onehot_rows, ROWS)
+    @pl.loop(0, 8)
+    def _(pair):
+        for block in (2 * pair, 2 * pair + 1):
+            spread(lines[0, :, 0:nnz], block, lines[1, :, 0:nnz], onehot_rows, 0)
+            spread(lines[0, :, 0:nnz], block, lines[2, :, 0:nnz], onehot_rows, ROWS)
 
     def tabulate(start, stop):
         @pl.loop(start, stop)
         def _(field):
-            @pl.loop(0, 16)
-            def _(block):
+            @pl.loop(0, 4)
+            def _(four):
                 ones = jnp.ones((16, nnz), bf16)
-                spread(lines[3 + field, :, 0:nnz], block, ones, onehot_cols, 0)
+                for block in range(4):
+                    spread(lines[3 + field, :, 0:nnz], 4 * four + block, ones, onehot_cols, 0)
 
             pieces = lax.dot_general(
                 onehot_rows[...], onehot_cols[...], (((1,), (1,)), ((), ())), preferred_element_type=f32
@@ -362,7 +365,7 @@
                             end = WIN
                         drops[face, to, first + begin : first + end] = drop[:, begin:end]
 
-        @pl.when(group >= 0)
+        @pl.when(part >= 0)
         def _():
             for first in range(0, FLAT, 256):
                 lanes = slice(first, min(first + 256, FLAT))
@@ -387,16 +390,29 @@
             own_middle.wait()
         scale_group(x1, group)
     combine(y1, 0)
+    for group in range(groups):
+        start_low(y_planes(group)[0])
+    combine(y1, 512)
+
     for step in range(groups):
-        start_low(y_planes(group_of(step))[0])
-    combine(y1, 512)
-
-    for step in range(groups):
-        start_high(y_planes(group_of(step))[1])
-
-    @pl.loop(0, 16)
-    def _(block):
-        at = pl.ds(pl.multiple_of(block * 16, 16), 16)
+        start_high(y_planes(step)[1])
+
+    def row_copy(source, target, index, other, group):
+        rows = rows_of(group)
+        return pltpu.make_async_remote_copy(
+            src_ref=source.at[rows, :], dst_ref=target.at[rows, :],
+            send_sem=h_send.at[index * groups + group], recv_sem=h_recv.at[index * groups + group],
+            device_id=(other, slab), device_id_type=MESH,
+        )
+
+    def rows_left(group):
+        return row_copy(edge_high, halo_high, 0, part - 1, group)
+
+    def rows_right(group):
+        return row_copy(edge_low, halo_low, 1, part + 1, group)
+
+    for group in range(groups):
+        at = pl.ds(group * PAD, PAD)
         tile = [y1[at, t * 128 : t * 128 + 128].astype(f32) for t in range(7)]
         up = [pltpu.roll(tile[t], 32, 1) for t in (0, 4, 2)]
         edge_high[at, 0:128] = jnp.where((tile_lane >= 32) & (tile_lane < 80), up[0], up[1]).astype(bf16)
@@ -406,17 +422,8 @@
             tile_lane >= 96, down[1], jnp.where(tile_lane >= 80, down[0], down[2])
         ).astype(bf16)
         edge_low[at, 128:256] = down[3].astype(bf16)
-
-    def row_copy(source, target, index, other):
-        return pltpu.make_async_remote_copy(
-            src_ref=source, dst_ref=target, send_sem=h_send.at[index],
-            recv_sem=h_recv.at[index], device_id=(other, slab), device_id_type=MESH,
-        )
-
-    rows_left = lambda: row_copy(edge_high, halo_high, 0, part - 1)
-    rows_right = lambda: row_copy(edge_low, halo_low, 1, part + 1)
-    pl.when(left)(lambda: rows_left().start())
-    pl.when(right)(lambda: rows_right().start())
+        pl.when(left)(lambda: rows_left(group).start())
+        pl.when(right)(lambda: rows_right(group).start())
 
     def out_copy(y, land, peer, source, sems, lanes=(0, FLAT), shift=0):
         window = pl.ds(lanes[0], lanes[1])
@@ -439,16 +446,8 @@
             out_copy(y, land, part, group_of(step), sems, *how).wait_recv()
 
     o1_sems, o2_sems = (o1_send, o1_recv), (o2_send, o2_recv)
-    pl.when(left)(lambda: rows_right().wait_recv())
-    pl.when(right)(lambda: rows_left().wait_recv())
-
-    start_out(y1, land1, o1_sems)
-    own1 = pltpu.make_async_copy(y1.at[rows_of(part), :], land1.at[part], self_sem)
-    own1.start()
-
-    @pl.loop(0, 16)
-    def _(block):
-        at = pl.ds(pl.multiple_of(block * 16, 16), 16)
+    def windows(group):
+        at = pl.ds(group * PAD, PAD)
         tile = [y1[at, t * 128 : t * 128 + 128].astype(f32) for t in (2, 4, 6)]
         high, high_b = (halo_high[at, t : t + 128].astype(f32) for t in (0, 128))
         low, low_b = (halo_low[at, t : t + 128].astype(f32) for t in (0, 128))
@@ -467,8 +466,14 @@
         x2[2, at, 128:256] = y1[at, 640:768]
         x2[2, at, 256:384] = jnp.where(tile_lane < 96, tile[2], high).astype(bf16)
 
-    for step in range(groups):
-        group = group_of(step)
+    own1 = pltpu.make_async_copy(y1.at[rows_of(part), :], land1.at[part], self_sem)
+    for group in range(groups):
+        pl.when(left)(lambda: rows_right(group).wait_recv())
+        pl.when(right)(lambda: rows_left(group).wait_recv())
+        windows(group)
+        if group == OUT1:
+            start_out(y1, land1, o1_sems)
+            own1.start()
         arrive_planes(*y_planes(group))
         scale_group(x2, group)
     begin, end = ((0, 512), 0), ((512, FLAT - 512), groups)
@@ -480,8 +485,8 @@
     own2 = pltpu.make_async_copy(y2.at[rows_of(part), :], land2.at[part], self_sem)
     own2.start()
 
-    def assemble(land, out_ref):
-        for plane in range(3):
+    def assemble(land, out_ref, planes):
+        for plane in planes:
             carry = None
             for source in range(groups):
                 tile, offset = divmod(CELLS * source, 128)
@@ -499,23 +504,24 @@
                     out_ref[plane, :, tile * 128 + 256 : tile * 128 + 384] = carry.astype(bf16)
 
     arrive_out(y1, land1, o1_sems)
-    assemble(land1, first_ref)
+    assemble(land1, first_ref, range(3))
 
     leave_planes(*coef_copies)
     for step in range(groups):
         leave_planes(*x_planes(group_of(step)))
-        leave_planes(*y_planes(group_of(step)))
+        leave_planes(*y_planes(step))
+        pl.when(left)(lambda: rows_left(step).wait_send())
+        pl.when(right)(lambda: rows_right(step).wait_send())
     for step in range(1, groups):
         a2a(group_of(step), part).wait_send()
         a2a_middle(group_of(step), part).wait_send()
-    pl.when(left)(lambda: rows_left().wait_send())
-    pl.when(right)(lambda: rows_right().wait_send())
     leave_out(y1, land1, o1_sems)
 
     own2.wait()
-    for how in (begin, end):
-        arrive_out(y2, land2, o2_sems, *how)
-    assemble(land2, second_ref)
+    arrive_out(y2, land2, o2_sems, *begin)
+    assemble(land2, second_ref, (0,))
+    arrive_out(y2, land2, o2_sems, *end)
+    assemble(land2, second_ref, (1, 2))
     for how in (begin, end):
         leave_out(y2, land2, o2_sems, *how)
 
@@ -565,7 +571,7 @@
             pltpu.VMEM((ROWS, fields * ROWS), bf16),
             pltpu.VMEM((fields * ROWS, FLAT), bf16),
             dma((groups,)), dma((groups,)), dma((groups,)), dma((groups,)), dma, dma,
-            dma((2 * groups,)), dma((2 * groups,)), dma((2,)), dma((2,)), dma((2,)), dma((2,)),
+            dma((2 * groups,)), dma((2 * groups,)), dma((2,)), dma((2,)), dma((2 * groups,)), dma((2 * groups,)),
             dma((groups,)), dma((groups,)), dma((2 * groups,)), dma((2 * groups,)),
             dma((2 * groups,)), dma((2 * groups,)),
         ],

time: 41.5 us -> 39.9 us (0.961)
  Pallas kernels: 39.2 us -> 37.6 us
    pallas_call x1, Pallas kernels: 39.2 us -> 37.6 us  [shards(): pl.pallas_call(functools.partial(kernel, groups, slabs, fields, nnz), out...]
where the time goes in v4:
time: 39.9 us; the launch traced here: 39.7 us
  Pallas kernels  37.6 us (94%)
  local copies, waits for them, and re-layouts  1.53 us (4%)
  between operations  0.64 us (2%)
    pallas_call x1, Pallas kernels, shards(): pl.pallas_call(functools.partial(kernel, groups, slabs, fields, nnz), out...  37.6 us
    unnamed x2, local copies, waits for them, and re-layouts  1.53 us

profile of v4, /device:TPU:7, one launch (start us, length us, event | category | flops | bytes accessed | tf_op | source)
XLA Modules:
  0.0 39.7 jit_solution(15001248290121767234)
XLA Ops:
  0.6 37.6 %shard_map.77 = (bf16[3,27,2304]{2,1,0:T(8,128)(2,1)S(1)}, bf16[3,27,2304]{2,1,0:T(8,128)(2,1)S(1)}) custom-call(bf16[3,27,2304]{2,1,0:T(8,128)(2,1)} %bitcast.6, f32[3,2304]{1,0:T(4,128)} %mean_hbm.1, f32[6,3,2304]{2,1,0:T(4,128)} %fluct_hbm.1, s32[3,1218]{1,0:T(4,128)} %bitcast.7, f32[1218]{0:T(1024)} %product_hbm.1, s32[210]{0:T(256)} %slot_hbm.1), custom_call_target="tpu_custom_call" | custom-call | tf_op jit(solution)/shard_map/pallas_call | solution.py:538
  38.2 0.8 %copy.10 = bf16[27,3,2304]{2,0,1:T(8,128)(2,1)} copy(bf16[27,3,2304]{2,0,1:T(8,128)(2,1)S(1)} %bitcast.5) | data formatting | bytes 746496
  39.0 0.8 %copy.11 = bf16[27,3,2304]{2,0,1:T(8,128)(2,1)} copy(bf16[27,3,2304]{2,0,1:T(8,128)(2,1)S(1)} %bitcast.4) | data formatting | bytes 746496

commit v5 on v4

--- a/solution.py
+++ b/solution.py
@@ -18,7 +18,7 @@
 
 AT = (0, 2, 1)
 SEND = (1, 2, 3, 4, 6, 5, 7)
-OUT1 = 2
+OUT1 = 1
 
 ORDER = ((0, 0), (0, 1), (2, 0), (2, 1), (1, 0), (1, 1), (3, 0), (3, 1))
 
@@ -291,14 +291,12 @@
                 pieces[0:ROWS] + pieces[ROWS:]
             ).astype(bf16)
 
-    tabulate(0, 2)
+    tabulate(0, 3)
     pass_on(1)
-    tabulate(2, 4)
-    pass_on(2)
-    pass_on(3)
-    tabulate(4, 6)
-    pass_on(4)
-    pass_on(6)
+    tabulate(3, 5)
+    for step in (2, 3, 4, 6):
+        pass_on(step)
+    tabulate(5, 6)
 
     arrive_planes(*coef_copies)
     inside = []

time: 39.9 us -> 38.7 us (0.970)
  Pallas kernels: 37.6 us -> 36.4 us
    pallas_call x1, Pallas kernels: 37.6 us -> 36.4 us  [shards(): pl.pallas_call(functools.partial(kernel, groups, slabs, fields, nnz), out...]
where the time goes in v5:
time: 38.7 us; the launch traced here: 38.6 us
  Pallas kernels  36.4 us (94%)
  local copies, waits for them, and re-layouts  1.53 us (4%)
  between operations  0.64 us (2%)
    pallas_call x1, Pallas kernels, shards(): pl.pallas_call(functools.partial(kernel, groups, slabs, fields, nnz), out...  36.4 us
    unnamed x2, local copies, waits for them, and re-layouts  1.53 us

profile of v5, /device:TPU:7, one launch (start us, length us, event | category | flops | bytes accessed | tf_op | source)
XLA Modules:
  0.0 38.6 jit_solution(12816978260822904023)
XLA Ops:
  0.6 36.4 %shard_map.77 = (bf16[3,27,2304]{2,1,0:T(8,128)(2,1)S(1)}, bf16[3,27,2304]{2,1,0:T(8,128)(2,1)S(1)}) custom-call(bf16[3,27,2304]{2,1,0:T(8,128)(2,1)} %bitcast.6, f32[3,2304]{1,0:T(4,128)} %mean_hbm.1, f32[6,3,2304]{2,1,0:T(4,128)} %fluct_hbm.1, s32[3,1218]{1,0:T(4,128)} %bitcast.7, f32[1218]{0:T(1024)} %product_hbm.1, s32[210]{0:T(256)} %slot_hbm.1), custom_call_target="tpu_custom_call" | custom-call | tf_op jit(solution)/shard_map/pallas_call | solution.py:536
  37.0 0.8 %copy.10 = bf16[27,3,2304]{2,0,1:T(8,128)(2,1)} copy(bf16[27,3,2304]{2,0,1:T(8,128)(2,1)S(1)} %bitcast.5) | data formatting | bytes 746496
  37.8 0.8 %copy.11 = bf16[27,3,2304]{2,0,1:T(8,128)(2,1)} copy(bf16[27,3,2304]{2,0,1:T(8,128)(2,1)S(1)} %bitcast.4) | data formatting | bytes 746496

commit v6 on v5

--- a/solution.py
+++ b/solution.py
@@ -18,7 +18,7 @@
 
 AT = (0, 2, 1)
 SEND = (1, 2, 3, 4, 6, 5, 7)
-OUT1 = 1
+OUT1 = 0
 
 ORDER = ((0, 0), (0, 1), (2, 0), (2, 1), (1, 0), (1, 1), (3, 0), (3, 1))
 

time: 38.7 us -> 37.8 us (0.977)
  Pallas kernels: 36.4 us -> 35.5 us
    pallas_call x1, Pallas kernels: 36.4 us -> 35.5 us  [shards(): pl.pallas_call(functools.partial(kernel, groups, slabs, fields, nnz), out...]
where the time goes in v6:
time: 37.8 us; the launch traced here: 37.6 us
  Pallas kernels  35.5 us (94%)
  local copies, waits for them, and re-layouts  1.53 us (4%)
  between operations  0.64 us (2%)
    pallas_call x1, Pallas kernels, shards(): pl.pallas_call(functools.partial(kernel, groups, slabs, fields, nnz), out...  35.5 us
    unnamed x2, local copies, waits for them, and re-layouts  1.53 us

profile of v6, /device:TPU:7, one launch (start us, length us, event | category | flops | bytes accessed | tf_op | source)
XLA Modules:
  0.0 37.6 jit_solution(10810097235459944518)
XLA Ops:
  0.6 35.5 %shard_map.77 = (bf16[3,27,2304]{2,1,0:T(8,128)(2,1)S(1)}, bf16[3,27,2304]{2,1,0:T(8,128)(2,1)S(1)}) custom-call(bf16[3,27,2304]{2,1,0:T(8,128)(2,1)} %bitcast.6, f32[3,2304]{1,0:T(4,128)} %mean_hbm.1, f32[6,3,2304]{2,1,0:T(4,128)} %fluct_hbm.1, s32[3,1218]{1,0:T(4,128)} %bitcast.7, f32[1218]{0:T(1024)} %product_hbm.1, s32[210]{0:T(256)} %slot_hbm.1), custom_call_target="tpu_custom_call" | custom-call | tf_op jit(solution)/shard_map/pallas_call | solution.py:536
  36.1 0.8 %copy.10 = bf16[27,3,2304]{2,0,1:T(8,128)(2,1)} copy(bf16[27,3,2304]{2,0,1:T(8,128)(2,1)S(1)} %bitcast.5) | data formatting | bytes 746496
  36.9 0.8 %copy.11 = bf16[27,3,2304]{2,0,1:T(8,128)(2,1)} copy(bf16[27,3,2304]{2,0,1:T(8,128)(2,1)S(1)} %bitcast.4) | data formatting | bytes 746496
